TPU v7x, 512 devices: a whole 4x8x8 slice. The times are simulated.
512 devices in a mesh: pair: 32 (over y, x), row: 16 (over z, core).
Axes of the slice: x: 4, y: 8, z: 8, core: 2. Of those that a mesh axis runs over, the one named last changes fastest.
Arguments:
- r_factor: float32 [16384, 16384], P(('row', 'pair')), may hold values from -40 to 40, as said below
- block_slots: int32 [256], replicated, may hold values from 0 to 255, as said below
Outputs:
- rotated: float32 [16384, 16384], P('row', 'pair')
- off_ratio: float32 [], replicated
Inputs may be any that keep to these rules, and one draw needn't show every extreme that they name: `block_slots`: each of the 256 column blocks appears exactly once. `r_factor`: entries below the diagonal are zero and the diagonal is positive.
All inputs are finite; a program needn't handle non-finite values.
Results may differ from a plain program's by a relative error of at most 0.0001.
Values sent between devices are 32-bit elements; how exact they have to be, the bound alone decides.
A program may use at most 64 MiB of HBM per device.

v0:
```python
import jax
import jax.numpy as jnp
from jax import lax
from jax.sharding import PartitionSpec as P

BLOCK = 64
ITERS = 3


def passed_along(value, axis, by):
    count = lax.axis_size(axis)
    pairs = [(i, i + by) for i in range(count) if 0 <= i + by < count]
    return lax.ppermute(value, axis, pairs)


def cayley(pair_gram):
    size_n = pair_gram.shape[0]
    diag_vals = jnp.diagonal(pair_gram)
    spread = diag_vals[:, None] - diag_vals[None, :]
    denom = 2.0 * (diag_vals[:, None] ** 2 + diag_vals[None, :] ** 2)
    skew_part = pair_gram * spread / denom
    unit_matrix = jnp.eye(size_n, dtype=pair_gram.dtype)
    minus_part = unit_matrix - skew_part
    system = unit_matrix - jnp.dot(skew_part, skew_part, precision=lax.Precision.HIGHEST)
    product = jnp.dot(minus_part, minus_part, precision=lax.Precision.HIGHEST)
    factor = jnp.linalg.cholesky(system)
    return jax.scipy.linalg.cho_solve((factor, True), product.T).T


def square_sums(rows_part):
    row_ids = jnp.arange(rows_part.shape[1], dtype=jnp.int32)[:, None]
    col_ids = jnp.arange(rows_part.shape[2], dtype=jnp.int32)[None, :]
    on_diag = (row_ids == col_ids)[None, :, :]
    squares = rows_part * rows_part
    return (jnp.sum(jnp.where(on_diag, 0.0, squares)), jnp.sum(jnp.where(on_diag, squares, 0.0)))


def on_device(r_factor, block_slots):
    rows_in, total_cols = r_factor.shape
    blocks = total_cols // BLOCK
    pair_width = 2 * BLOCK
    arranged = jnp.take(r_factor.reshape(rows_in, blocks, BLOCK), block_slots, axis=1)
    arranged = arranged.reshape(rows_in, blocks // 2, pair_width)
    received = lax.all_to_all(arranged, "pair", split_axis=1, concat_axis=0, tiled=True)
    column = jnp.transpose(received, (1, 0, 2))
    local_pairs = column.shape[0]
    rows_here = column.shape[1]
    totals = None
    for sweep in range(ITERS):
        partial_value = jnp.einsum("pri,prj->pij", column, column, precision=lax.Precision.HIGHEST)
        pair_gram = lax.psum(partial_value, "row")
        if sweep == 0:
            off_part, diag_part = square_sums(pair_gram)
            totals = lax.psum((off_part, diag_part), "pair")
        rotation = jax.vmap(cayley)(pair_gram)
        column = jnp.einsum("pri,pij->prj", column, rotation, precision=lax.Precision.HIGHEST)
    upper_half = column[:, :, :BLOCK]
    lower_half = column[:, :, BLOCK:]
    pair_index = lax.axis_index("pair")
    pair_count = lax.axis_size("pair")
    global_ids = pair_index * local_pairs + jnp.arange(local_pairs, dtype=jnp.int32)
    last_id = pair_count * local_pairs - 1
    first_mask = (global_ids == 0)[:, None, None]
    last_mask = (global_ids == last_id)[:, None, None]
    forward = jnp.where(first_mask, lower_half, upper_half)
    came_up = passed_along(forward[local_pairs - 1], "pair", 1)
    came_down = passed_along(lower_half[0], "pair", -1)
    before = jnp.concatenate([came_up[None], forward[: local_pairs - 1]], axis=0)
    after = jnp.concatenate([lower_half[1:], came_down[None]], axis=0)
    new_upper = jnp.where(first_mask, upper_half, before)
    new_lower = jnp.where(last_mask, upper_half, after)
    joined = jnp.concatenate([new_upper, new_lower], axis=2)
    rotated = jnp.transpose(joined, (1, 0, 2)).reshape(rows_here, local_pairs * pair_width)
    off_ratio = jnp.sqrt(totals[0] / totals[1])
    return (rotated, off_ratio)


def solution(mesh):
    in_specs = (P(("row", "pair"), None), P())
    out_specs = (P("row", "pair"), P())
    return jax.shard_map(
        on_device, mesh=mesh, in_specs=in_specs, out_specs=out_specs, check_vma=False
    )
```

profile of v0, /device:TPU:32, one launch (start us, length us, event | category | flops | bytes accessed | tf_op | source)
XLA Modules:
  0.0 870.0 jit_solution(1644041194459896223)
XLA Ops:
  7.2 0.7 compare_and_fusion
  7.9 0.7 compare_select_fusion
  8.5 0.2 broadcast_in_dim.98
  8.9 4.3 reshape.87
  13.2 6.5 copy.172
  19.7 5.0 gather_fusion
  24.7 6.5 copy.173
  31.3 3.3 gather.17
  34.5 0.2 broadcast_select_fusion
  34.7 2.5 copy.174
  37.3 9.8 %all-to-all-start = ((f32[32,128,128]{2,0,1:T(8,128)}), f32[32,128,128]{2,0,1:T(8,128)S(1)}, u32[]{:S(2)}, u32[]{:S(2)}) async-start(f32[32,128,128]{2,0,1:T(8,128)} %copy.174), calls=%async_computation | async-start | bytes 4194304 | tf_op jit(solution)/shard_map/all_to_all | solution.py:44
  47.1 0.3 all-reduce.5.cloned.1.call-start
  47.4 46.9 %all-to-all-done = f32[32,128,128]{2,0,1:T(8,128)S(1)} async-done(((f32[32,128,128]{2,0,1:T(8,128)}), f32[32,128,128]{2,0,1:T(8,128)S(1)}, u32[]{:S(2)}, u32[]{:S(2)}) %all-to-all-start) | async-done | bytes 2097184 | tf_op jit(solution)/shard_map/all_to_all | solution.py:44
  94.3 1.3 copy-done.3
  95.6 1.8 copy.175
  97.4 4.3 fusion.33
  101.8 119.5 %all-reduce.5.cloned.1.call-done = f32[4,128,128]{1,2,0:T(8,128)} async-done(((f32[4,128,128]{1,2,0:T(8,128)}), f32[4,128,128]{1,2,0:T(8,128)}) %all-reduce.5.cloned.1.call-update) | async-done | bytes 262160 | tf_op jit(solution)/shard_map/psum | solution.py:51
  221.3 8.5 copy.178
  229.7 1.8 gather_fusion.1
  231.6 0.7 convolution_subtract_fusion.2
  232.3 0.1 copy.183
  232.4 46.9 %custom-call.18 = f32[4,128,128]{2,1,0:T(8,128)S(1)} custom-call(f32[4,128,128]{2,1,0:T(8,128)S(1)} %fusion.14), custom_call_target="Cholesky" | custom-call | tf_op jit(solution)/shard_map/vmap(jit(cholesky))/cholesky | solution.py:26
  279.6 39.7 %custom-call.19 = f32[4,1,128,128]{2,3,1,0:T(8,128)S(1)} custom-call(f32[4,1,128,128]{3,2,1,0:T(8,128)S(1)} %select_bitcast_fusion.2), custom_call_target="InvertDiagBlocksLowerTriangular" | custom-call | tf_op jit(solution)/shard_map/vmap(jit(_cho_solve))/triangular_solve | solution.py:27
  319.3 0.6 fusion.19
  320.0 0.6 fusion.12
  320.6 0.4 fusion.10
  321.0 1.9 fusion.34
  323.0 1.3 copy-done
  324.3 4.3 fusion.35
  328.6 116.2 %all-reduce.7.cloned.1.call-done = f32[4,128,128]{1,2,0:T(8,128)} async-done(((f32[4,128,128]{1,2,0:T(8,128)}), f32[4,128,128]{1,2,0:T(8,128)}) %all-reduce.7.cloned.1.call-update) | async-done | bytes 262160 | tf_op jit(solution)/shard_map/psum | solution.py:51
  444.8 8.5 copy.188
  453.3 1.8 gather_fusion.2
  455.2 0.7 convolution_subtract_fusion.1
  455.9 0.1 copy.193
  456.0 46.9 %custom-call.20 = f32[4,128,128]{2,1,0:T(8,128)S(1)} custom-call(f32[4,128,128]{2,1,0:T(8,128)S(1)} %fusion.9), custom_call_target="Cholesky" | custom-call | tf_op jit(solution)/shard_map/vmap(jit(cholesky))/cholesky | solution.py:26
  503.2 39.5 %custom-call.21 = f32[4,1,128,128]{2,3,1,0:T(8,128)S(1)} custom-call(f32[4,1,128,128]{3,2,1,0:T(8,128)S(1)} %select_bitcast_fusion.1), custom_call_target="InvertDiagBlocksLowerTriangular" | custom-call | tf_op jit(solution)/shard_map/vmap(jit(_cho_solve))/triangular_solve | solution.py:27
  542.7 0.6 fusion.17
  543.4 0.6 fusion.7
  544.0 0.4 fusion.5
  544.4 3.5 fusion.36
  547.9 4.3 fusion.37
  552.2 116.0 %all-reduce.9.cloned.1.call-done = f32[4,128,128]{1,2,0:T(8,128)} async-done(((f32[4,128,128]{1,2,0:T(8,128)}), f32[4,128,128]{1,2,0:T(8,128)}) %all-reduce.9.cloned.1.call-update) | async-done | bytes 262160 | tf_op jit(solution)/shard_map/psum | solution.py:51
  668.3 8.5 copy.198
  676.7 1.8 gather_fusion.3
  678.6 0.7 convolution_subtract_fusion
  679.2 0.1 copy.203
  679.4 0.7 fusion.4
  680.1 47.9 %custom-call.22 = f32[4,128,128]{2,1,0:T(8,128)S(1)} custom-call(f32[4,128,128]{2,1,0:T(8,128)} %fusion.4), custom_call_target="Cholesky" | custom-call | tf_op jit(solution)/shard_map/vmap(jit(cholesky))/cholesky | solution.py:26
  728.3 39.3 %custom-call.23 = f32[4,1,128,128]{2,3,1,0:T(8,128)S(1)} custom-call(f32[4,1,128,128]{3,2,1,0:T(8,128)S(1)} %select_bitcast_fusion), custom_call_target="InvertDiagBlocksLowerTriangular" | custom-call | tf_op jit(solution)/shard_map/vmap(jit(_cho_solve))/triangular_solve | solution.py:27
  767.6 0.7 fusion.15
  768.3 0.6 fusion.2
  768.9 0.4 fusion
  769.3 2.0 fusion.38
  771.3 0.8 slice_bitcast_fusion
  772.1 4.6 collective-permute-start.1
  776.7 0.2 slice_select_fusion
  776.9 0.7 slice_bitcast_fusion.1
  777.6 1.9 collective-permute-start
  779.6 0.8 select_reduce_fusion.3
  780.4 75.6 %all-reduce = (f32[]{:T(128)}, f32[]{:T(128)}) all-reduce(f32[]{:T(128)} %get-tuple-element.15, f32[]{:T(128)} %get-tuple-element.14), channel_id=1, replica_groups=mesh['pair'=32,'row'=16] {'pair'}, use_global_device_ids=true, to_apply=%region_6.9 | all-reduce | flops 2 | bytes 16 | tf_op jit(solution)/shard_map/psum | solution.py:54
  857.2 1.2 slice.50
  858.5 1.4 maximum_select_fusion
  860.0 0.1 pad_maximum_fusion
  860.1 1.8 copy.206
  (48 shorter events, 1.6 us)
Async XLA Ops:
  37.3 57.0 %all-to-all-start = ((f32[32,128,128]{2,0,1:T(8,128)}), f32[32,128,128]{2,0,1:T(8,128)S(1)}, u32[]{:S(2)}, u32[]{:S(2)}) async-start(f32[32,128,128]{2,0,1:T(8,128)} %copy.174), calls=%async_computation | async-start | bytes 4194304 | tf_op jit(solution)/shard_map/all_to_all | solution.py:44
  47.1 174.2 %all-reduce.5.cloned.1.call-start = ((), (), s32[]{:S(2)}) async-start(), calls=%async_computation.1 | async-start | bytes 524288 | tf_op jit(solution)/shard_map/psum | solution.py:51
  94.3 1.3 copy-start.3
  101.7 343.1 %all-reduce.7.cloned.1.call-start = ((), (), s32[]{:S(2)}) async-start(), calls=%async_computation.2 | async-start | bytes 524288 | tf_op jit(solution)/shard_map/psum | solution.py:51
  221.3 10.3 %copy-start.4 = (f32[4,128,128]{1,2,0:T(8,128)S(1)}, f32[4,128,128]{1,2,0:T(8,128)}, u32[]{:S(2)}) copy-start(f32[4,128,128]{1,2,0:T(8,128)} %all-reduce.5.cloned.1.call-done) | copy-start | bytes 786436
  323.0 1.3 copy-start
  328.6 339.7 %all-reduce.9.cloned.1.call-start = ((), (), s32[]{:S(2)}) async-start(), calls=%async_computation.3 | async-start | bytes 524288 | tf_op jit(solution)/shard_map/psum | solution.py:51
  444.8 10.4 %copy-start.6 = (f32[4,128,128]{1,2,0:T(8,128)S(1)}, f32[4,128,128]{1,2,0:T(8,128)}, u32[]{:S(2)}) copy-start(f32[4,128,128]{1,2,0:T(8,128)} %all-reduce.7.cloned.1.call-done) | copy-start | bytes 786436
  668.3 10.3 %copy-start.5 = (f32[4,128,128]{1,2,0:T(8,128)S(1)}, f32[4,128,128]{1,2,0:T(8,128)}, u32[]{:S(2)}) copy-start(f32[4,128,128]{1,2,0:T(8,128)} %all-reduce.9.cloned.1.call-done) | copy-start | bytes 786436
  771.3 6.3 copy-start.1
  772.1 86.4 %collective-permute-start.1 = (f32[1024,64]{0,1:T(8,128)}, f32[1024,64]{0,1:T(8,128)}, u32[]{:S(2)}, u32[]{:S(2)}) collective-permute-start(f32[1024,64]{0,1:T(8,128)} %slice_bitcast_fusion), channel_id=1, source_target_pairs={{16,0},{32,16},{48,32},{64,48},{80,64},{96,80},{112,96},{128,112},... | collective-permute-start | bytes 786440 | tf_op jit(solution)/shard_map/ppermute | solution.py:13
  777.6 80.9 %collective-permute-start = (f32[1024,64]{0,1:T(8,128)}, f32[1024,64]{0,1:T(8,128)}, u32[]{:S(2)}, u32[]{:S(2)}) collective-permute-start(f32[1024,64]{0,1:T(8,128)} %slice_bitcast_fusion.1), channel_id=1, source_target_pairs={{0,16},{16,32},{32,48},{48,64},{64,80},{80,96},{96,112},{112,128},... | collective-permute-start | bytes 786440 | tf_op jit(solution)/shard_map/ppermute | solution.py:13
  779.5 79.0 %copy-start.2 = (f32[4,1024,128]{1,2,0:T(8,128)S(1)}, f32[4,1024,128]{1,2,0:T(8,128)}, u32[]{:S(2)}) copy-start(f32[4,1024,128]{1,2,0:T(8,128)} %copy-done.1) | copy-start | bytes 6291460
Sparse Core Ops, SparseCore 0:
  101.8 119.4 all-reduce.4
  328.7 116.0 all-reduce.6
  552.3 115.8 all-reduce.8
where the time goes:
time: 877 us; the launch traced here: 870 us
  waiting for transfers between devices  399 us (45%)
  other arithmetic  266 us (30%)
  blocking collectives  75.6 us (9%)
  local copies, waits for them, and re-layouts  68.9 us (8%)
  matrix products  27.1 us (3%)
  between operations  17 us (2%)
  starting transfers between devices  16.6 us (2%)
    psum x3, waiting for transfers between devices, on_device(): pair_gram = lax.psum(partial_value, 'row')  352 us
    another operation x10, other arithmetic, cayley(): factor = jnp.linalg.cholesky(system)  142 us
    another operation x7, other arithmetic, cayley(): return jax.scipy.linalg.cho_solve((factor, True), product.T).T  119 us
    psum x1, blocking collectives, on_device(): totals = lax.psum((off_part, diag_part), 'pair')  75.6 us
    all_to_all x1, waiting for transfers between devices, on_device(): lax.all_to_all(arranged, 'pair', split_axis=1, concat_axis=0, tiled=True)  46.9 us
    psum x3, local copies, waits for them, and re-layouts, on_device(): pair_gram = lax.psum(partial_value, 'row')  25.4 us
  transfers between devices with their start and end apart: 6, of which 4 were waited for; matrix products, arithmetic and copies ran while one was open for 0% of the time, Pallas kernels for 0%

commit v1 on v0

v1 whole, which is shorter than its diff:
```python
import functools

import jax
import jax.numpy as jnp
from jax import lax
from jax.experimental import pallas as pl
from jax.experimental.pallas import tpu as pltpu
from jax.sharding import PartitionSpec as P

BLOCK = 64
ITERS = 3
WIDTH = 2 * BLOCK
MESH = pl.DeviceIdType.MESH
HIGHEST = lax.Precision.HIGHEST
NEUMANN_TOL = 1e-8
X_CHIPS = 4


def mm(lhs, rhs, lhs_dim=1):
    return lax.dot_general(
        lhs,
        rhs,
        (((lhs_dim,), (0,)), ((), ())),
        precision=HIGHEST,
        preferred_element_type=jnp.float32,
    )


def lanes(shape):
    return lax.broadcasted_iota(jnp.int32, shape, len(shape) - 1)


def arrange_kernel(slots_ref, r_ref, out_ref):
    group = pl.program_id(0)
    rows = r_ref.shape[0]
    low = lanes((rows, WIDTH)) < BLOCK
    for pair in range(out_ref.shape[2] // WIDTH):
        halves = []
        for side in range(2):
            block = slots_ref[group * (out_ref.shape[2] // BLOCK) + 2 * pair + side]
            tile = r_ref[:, pl.ds(pl.multiple_of((block // 2) * WIDTH, WIDTH), WIDTH)]
            halves.append(pltpu.roll(tile, ((block + side) % 2) * BLOCK, 1))
        out_ref[0, :, pair * WIDTH : (pair + 1) * WIDTH] = jnp.where(low, halves[0], halves[1])


def arrange(r_factor, block_slots, groups):
    rows, cols = r_factor.shape
    return pl.pallas_call(
        arrange_kernel,
        out_shape=jax.ShapeDtypeStruct((groups, rows, cols // groups), jnp.float32),
        grid_spec=pltpu.PrefetchScalarGridSpec(
            num_scalar_prefetch=1,
            grid=(groups,),
            in_specs=[pl.BlockSpec((rows, cols), lambda g, s: (0, 0))],
            out_specs=pl.BlockSpec((1, rows, cols // groups), lambda g, s: (g, 0, 0)),
        ),
    )(block_slots, r_factor)


def gram_kernel(
    zs, x_ref, out_ref, part, half_in, mine, z_in, full,
    half_send, half_recv, rs_send, rs_recv, ag_send, ag_recv,
):
    row = lax.axis_index("row")
    z, core = row // 2, row % 2
    other = z * 2 + (1 - core)
    half = mine.shape[0]
    chunk = half // zs

    def peer(k):
        return lax.rem(z + k, zs)

    barrier = pltpu.get_barrier_semaphore()
    pl.semaphore_signal(barrier, inc=1, device_id={"row": other}, device_id_type=MESH)
    for k in range(1, zs):
        pl.semaphore_signal(
            barrier, inc=1, device_id={"row": peer(k) * 2 + core}, device_id_type=MESH
        )

    def gram(side):
        for i in range(half // WIDTH):
            at = pl.multiple_of(side * half + i * WIDTH, WIDTH)
            cols = x_ref[:, pl.ds(at, WIDTH)]
            part[pl.ds(at, WIDTH), :] = mm(cols, cols, 0)

    gram(1 - core)
    pl.semaphore_wait(barrier, zs)
    swap = pltpu.make_async_remote_copy(
        src_ref=part.at[pl.ds(pl.multiple_of((1 - core) * half, half), half)],
        dst_ref=half_in,
        send_sem=half_send,
        recv_sem=half_recv,
        device_id={"row": other},
        device_id_type=MESH,
    )
    swap.start()
    gram(core)
    swap.wait()
    mine[...] = part[pl.ds(pl.multiple_of(core * half, half), half), :] + half_in[...]

    def scatter(k):
        return pltpu.make_async_remote_copy(
            src_ref=mine.at[pl.ds(pl.multiple_of(peer(k) * chunk, chunk), chunk)],
            dst_ref=z_in.at[zs - k],
            send_sem=rs_send.at[k],
            recv_sem=rs_recv.at[zs - k],
            device_id={"row": peer(k) * 2 + core},
            device_id_type=MESH,
        )

    for k in range(1, zs):
        scatter(k).start()
    own = pl.ds(pl.multiple_of(z * chunk, chunk), chunk)
    for k in range(1, zs):
        scatter(k).wait()
    total = mine[own, :]
    for k in range(1, zs):
        total = total + z_in[k]
    full[own, :] = total

    def gather(k):
        return pltpu.make_async_remote_copy(
            src_ref=full.at[own],
            dst_ref=full.at[own],
            send_sem=ag_send.at[k],
            recv_sem=ag_recv.at[zs - k],
            device_id={"row": peer(k) * 2 + core},
            device_id_type=MESH,
        )

    for k in range(1, zs):
        gather(k).start()
    for k in range(1, zs):
        gather(k).wait()
    out_ref[...] = full[...]


def half_grams(column):
    rows, cols = column.shape
    half = cols // 2
    zs = lax.axis_size("row") // 2
    vmem = pl.BlockSpec(memory_space=pltpu.VMEM)
    dma = pltpu.SemaphoreType.DMA
    return pl.pallas_call(
        functools.partial(gram_kernel, zs),
        out_shape=jax.ShapeDtypeStruct((half, WIDTH), jnp.float32),
        in_specs=[vmem],
        out_specs=vmem,
        scratch_shapes=[
            pltpu.VMEM((cols, WIDTH), jnp.float32),
            pltpu.VMEM((half, WIDTH), jnp.float32),
            pltpu.VMEM((half, WIDTH), jnp.float32),
            pltpu.VMEM((zs, half // zs, WIDTH), jnp.float32),
            pltpu.VMEM((half, WIDTH), jnp.float32),
            dma,
            dma,
            dma((zs,)),
            dma((zs,)),
            dma((zs,)),
            dma((zs,)),
        ],
        compiler_params=pltpu.CompilerParams(collective_id=0, has_side_effects=True),
    )(column)


def rotation_kernel(g_ref, out_ref, gram, basis, power, turn):
    pairs = gram.shape[0]
    row_ids = lax.broadcasted_iota(jnp.int32, (WIDTH, WIDTH), 0)
    unit = row_ids == lanes((WIDTH, WIDTH))
    eye = jnp.where(unit, 1.0, 0.0).astype(jnp.float32)
    off = jnp.zeros((1, WIDTH), jnp.float32)
    on = jnp.zeros((1, WIDTH), jnp.float32)
    for p in range(pairs):
        value = g_ref[p * WIDTH : (p + 1) * WIDTH, :]
        gram[p] = value
        squares = value * value
        off = off + jnp.sum(jnp.where(unit, 0.0, squares), axis=0, keepdims=True)
        on = on + jnp.sum(jnp.where(unit, squares, 0.0), axis=0, keepdims=True)
    tile_row = lax.broadcasted_iota(jnp.int32, (8, WIDTH), 0)
    out_ref[pairs * WIDTH : pairs * WIDTH + 8, :] = jnp.where(
        tile_row == 0, off, jnp.where(tile_row == 1, on, 0.0)
    )

    for sweep in range(ITERS):
        ratio = jnp.zeros((), jnp.float32)
        for p in range(pairs):
            value = gram[p]
            on_diag = jnp.where(unit, value, 0.0)
            d_col = jnp.sum(on_diag, axis=1, keepdims=True)
            d_row = jnp.sum(on_diag, axis=0, keepdims=True)
            skew = value * (d_col - d_row) / (2.0 * (d_col * d_col + d_row * d_row))
            square = mm(skew, skew)
            bound = jnp.max(jnp.sum(jnp.abs(square), axis=0, keepdims=True))
            scale = 2.0 / (2.0 + bound)
            power[p] = eye - scale * (eye - square)
            turn[p] = scale * (eye - 2.0 * skew + square)
            ratio = jnp.maximum(ratio, bound / (2.0 + bound))

        def step(carry):
            for p in range(pairs):
                e = power[p]
                v = turn[p]
                turn[p] = v + mm(v, e)
                power[p] = mm(e, e)
            return carry * carry

        lax.while_loop(lambda left: left > NEUMANN_TOL, step, ratio)
        for p in range(pairs):
            v = turn[p]
            if sweep + 1 < ITERS:
                gram[p] = mm(v, mm(gram[p], v), 0)
            if sweep == 0:
                basis[p] = v
            elif sweep + 1 < ITERS:
                basis[p] = mm(basis[p], v)
            else:
                out_ref[p * WIDTH : (p + 1) * WIDTH, :] = mm(basis[p], v)


def rotations(grams):
    vmem = pl.BlockSpec(memory_space=pltpu.VMEM)
    pairs = grams.shape[0] // WIDTH
    work = pltpu.VMEM((pairs, WIDTH, WIDTH), jnp.float32)
    return pl.pallas_call(
        rotation_kernel,
        out_shape=jax.ShapeDtypeStruct((grams.shape[0] + 8, WIDTH), jnp.float32),
        in_specs=[vmem],
        out_specs=vmem,
        scratch_shapes=[work] * 4,
    )(grams)


def apply_kernel(
    xs, ys, x_ref, v_ref, out_ref, ratio_ref,
    v_in, turned, packed, landed, sum_x, sum_y,
    v_send, v_recv, edge_send, edge_recv, x_send, x_recv, y_send, y_recv,
):
    pair = lax.axis_index("pair")
    row = lax.axis_index("row")
    core = row % 2
    other = (row // 2) * 2 + (1 - core)
    count = xs * ys
    y, x = pair // xs, pair % xs
    rows = x_ref.shape[0]
    half = rows // 2
    vrows = v_ref.shape[0] - 8

    def x_peer(k):
        return y * xs + lax.rem(x + k, xs)

    def y_peer(k):
        return lax.rem(y + k, ys) * xs + x

    right, left = lax.rem(pair + 1, count), lax.rem(pair + count - 1, count)
    barrier = pltpu.get_barrier_semaphore()
    pl.semaphore_signal(barrier, inc=1, device_id={"row": other}, device_id_type=MESH)
    peers = [left, right] + [x_peer(k) for k in range(1, xs)] + [y_peer(k) for k in range(1, ys)]
    for peer in peers:
        pl.semaphore_signal(barrier, inc=1, device_id={"pair": peer}, device_id_type=MESH)

    def turn(source, j, local):
        v = source[pl.ds(pl.multiple_of(local * WIDTH, WIDTH), WIDTH), :]
        turned[j] = mm(x_ref[:, pl.ds(pl.multiple_of(j * WIDTH, WIDTH), WIDTH)], v)

    lane = lanes((half, WIDTH))

    def edge(side):
        value = turned.at[3 * side]
        keep = (lane < BLOCK) == (side == 1)
        packed[side] = jnp.where(keep, value[0:half, :], pltpu.roll(value[half:rows, :], BLOCK, 1))

    def edge_copy(side):
        return pltpu.make_async_remote_copy(
            src_ref=packed.at[side],
            dst_ref=landed.at[side],
            send_sem=edge_send.at[side],
            recv_sem=edge_recv.at[side],
            device_id={"pair": lax.rem(pair + count + 2 * side - 1, count)},
            device_id_type=MESH,
        )

    away = 1 - core
    turn(v_ref, 3 * core, core)
    edge(core)
    pl.semaphore_wait(barrier, len(peers) + 1)
    swap = pltpu.make_async_remote_copy(
        src_ref=v_ref,
        dst_ref=v_in,
        send_sem=v_send,
        recv_sem=v_recv,
        device_id={"row": other},
        device_id_type=MESH,
    )
    swap.start()
    edge_copy(core).start()
    turn(v_ref, 1 + core, away)
    swap.wait()
    turn(v_in, 3 * away, away)
    edge(away)
    edge_copy(away).start()

    sum_x[x] = v_ref[vrows : vrows + 8, :] + v_in[vrows : vrows + 8, :]

    def x_copy(k):
        return pltpu.make_async_remote_copy(
            src_ref=sum_x.at[x],
            dst_ref=sum_x.at[x],
            send_sem=x_send.at[k],
            recv_sem=x_recv.at[xs - k],
            device_id={"pair": x_peer(k)},
            device_id_type=MESH,
        )

    for k in range(1, xs):
        x_copy(k).start()
    turn(v_in, 2 - core, core)
    for k in range(1, xs):
        x_copy(k).wait()
    total = sum_x[0]
    for k in range(1, xs):
        total = total + sum_x[k]
    sum_y[y] = total

    def y_copy(k):
        return pltpu.make_async_remote_copy(
            src_ref=sum_y.at[y],
            dst_ref=sum_y.at[y],
            send_sem=y_send.at[k],
            recv_sem=y_recv.at[ys - k],
            device_id={"pair": y_peer(k)},
            device_id_type=MESH,
        )

    for k in range(1, ys):
        y_copy(k).start()

    low = lanes((rows, WIDTH)) < BLOCK
    first, last = pair == 0, pair == count - 1
    out_ref[:, 2 * WIDTH : 3 * WIDTH] = jnp.where(low, turned[1], turned[3])
    upper = jnp.where(first, pltpu.roll(turned[0], BLOCK, 1), turned[0])
    out_ref[:, WIDTH : 2 * WIDTH] = jnp.where(low, upper, turned[2])

    for k in range(1, ys):
        y_copy(k).wait()
    total = sum_y[0]
    for k in range(1, ys):
        total = total + sum_y[k]
    off = jnp.sum(total[0:1, :], axis=1, keepdims=True)
    on = jnp.sum(total[1:2, :], axis=1, keepdims=True)
    ratio_ref[...] = jnp.broadcast_to(jnp.sqrt(off / on), ratio_ref.shape)

    edge_copy(core).wait()
    edge_copy(away).wait()
    down = jnp.concatenate([landed[0], pltpu.roll(landed[0], BLOCK, 1)], axis=0)
    down = jnp.where(last, pltpu.roll(turned[3], BLOCK, 1), down)
    out_ref[:, 3 * WIDTH : 4 * WIDTH] = jnp.where(low, turned[2], down)
    up = jnp.concatenate([landed[1], pltpu.roll(landed[1], BLOCK, 1)], axis=0)
    up = jnp.where(first, turned[0], up)
    out_ref[:, 0:WIDTH] = jnp.where(low, up, turned[1])


def apply_and_move(column, turns):
    rows, cols = column.shape
    count = lax.axis_size("pair")
    xs = X_CHIPS
    ys = count // xs
    vmem = pl.BlockSpec(memory_space=pltpu.VMEM)
    dma = pltpu.SemaphoreType.DMA
    return pl.pallas_call(
        functools.partial(apply_kernel, xs, ys),
        out_shape=(
            jax.ShapeDtypeStruct((rows, cols), jnp.float32),
            jax.ShapeDtypeStruct((8, WIDTH), jnp.float32),
        ),
        in_specs=[vmem, vmem],
        out_specs=(vmem, vmem),
        scratch_shapes=[
            pltpu.VMEM(turns.shape, jnp.float32),
            pltpu.VMEM((cols // WIDTH, rows, WIDTH), jnp.float32),
            pltpu.VMEM((2, rows // 2, WIDTH), jnp.float32),
            pltpu.VMEM((2, rows // 2, WIDTH), jnp.float32),
            pltpu.VMEM((xs, 8, WIDTH), jnp.float32),
            pltpu.VMEM((ys, 8, WIDTH), jnp.float32),
            dma,
            dma,
            dma((2,)),
            dma((2,)),
            dma((xs,)),
            dma((xs,)),
            dma((ys,)),
            dma((ys,)),
        ],
        compiler_params=pltpu.CompilerParams(collective_id=1, has_side_effects=True),
    )(column, turns)


def on_device(r_factor, block_slots):
    rows_in, total_cols = r_factor.shape
    count = lax.axis_size("pair")
    slabs = arrange(r_factor, block_slots, count)
    received = lax.all_to_all(slabs, "pair", split_axis=0, concat_axis=0, tiled=True)
    column = received.reshape(rows_in * count, total_cols // count)
    turns = rotations(half_grams(column))
    rotated, ratio = apply_and_move(column, turns)
    return (rotated, ratio[0, 0])


def solution(mesh):
    in_specs = (P(("row", "pair"), None), P())
    out_specs = (P("row", "pair"), P())
    return jax.shard_map(
        on_device, mesh=mesh, in_specs=in_specs, out_specs=out_specs, check_vma=False
    )
```

time: 877 us -> 135 us (0.15)
  the two profiles are of different devices: /device:TPU:32 before, /device:TPU:1 now
where the time goes in v1:
time: 135 us; the launch traced here: 134 us
  Pallas kernels  70 us (52%)
  blocking collectives  59.3 us (44%)
  local copies, waits for them, and re-layouts  4.26 us (3%)
    all_to_all x1, blocking collectives, on_device(): lax.all_to_all(slabs, 'pair', split_axis=0, concat_axis=0, tiled=True)  59.3 us
    pallas_call x1, Pallas kernels, half_grams(): pl.pallas_call(functools.partial(gram_kernel, zs), out_shape=jax.ShapeDty...  26.3 us
    pallas_call x1, Pallas kernels, apply_and_move(): pl.pallas_call(functools.partial(apply_kernel, xs, ys), out_shape=(jax.Sh...  22.5 us
    pallas_call x1, Pallas kernels, arrange(): pl.pallas_call(arrange_kernel, out_shape=jax.ShapeDtypeStruct((groups, ro...  14.3 us
    pallas_call x1, Pallas kernels, rotations(): pl.pallas_call(rotation_kernel, out_shape=jax.ShapeDtypeStruct((grams.sha...  6.88 us
    unnamed x1, local copies, waits for them, and re-layouts  3.08 us

profile of v1, /device:TPU:1, one launch (start us, length us, event | category | flops | bytes accessed | tf_op | source)
XLA Modules:
  0.0 134.2 jit_solution(12718789403124501280)
XLA Ops:
  0.6 14.3 %shard_map.41 = f32[32,32,512]{2,1,0:T(8,128)} custom-call(s32[256]{0:T(256)} %slots_ref.1, f32[32,16384]{1,0:T(8,128)} %r_ref.1), custom_call_target="tpu_custom_call" | custom-call | tf_op jit(solution)/shard_map/pallas_call | solution.py:48
  14.9 59.3 %all_to_all.5 = f32[32,32,512]{2,1,0:T(8,128)} all-to-all(f32[32,32,512]{2,1,0:T(8,128)} %shard_map.41), channel_id=1, replica_groups=mesh['pair'=32,'row'=16] {'pair'}, dimensions={0} | all-to-all | bytes 4194304 | tf_op jit(solution)/shard_map/all_to_all | solution.py:401
  74.2 26.3 %shard_map.42.g_ref = f32[256,128]{1,0:T(8,128)} custom-call(f32[1024,512]{1,0:T(8,128)} %bitcast.2), custom_call_target="tpu_custom_call" | custom-call | tf_op jit(solution)/shard_map/pallas_call | solution.py:144
  100.5 6.9 %shard_map.43.v_ref = f32[264,128]{1,0:T(8,128)} custom-call(f32[256,128]{1,0:T(8,128)} %shard_map.42.g_ref), custom_call_target="tpu_custom_call" | custom-call | tf_op jit(solution)/shard_map/pallas_call | solution.py:224
  107.4 22.5 %shard_map.44 = (f32[1024,512]{1,0:T(8,128)}, f32[8,128]{1,0:T(8,128)}) custom-call(f32[1024,512]{1,0:T(8,128)} %bitcast.3, f32[264,128]{1,0:T(8,128)} %shard_map.43.v_ref), custom_call_target="tpu_custom_call" | custom-call | tf_op jit(solution)/shard_map/pallas_call | solution.py:369
  129.9 1.2 slice.3
  131.1 3.1 %copy.5 = f32[1024,512]{1,0:T(8,128)} copy(f32[1024,512]{1,0:T(8,128)} %get-tuple-element.8) | data formatting | bytes 4194304

commit v2 on v1

--- a/solution.py
+++ b/solution.py
@@ -14,6 +14,7 @@
 HIGHEST = lax.Precision.HIGHEST
 NEUMANN_TOL = 1e-8
 X_CHIPS = 4
+EARLY = 8
 
 
 def mm(lhs, rhs, lhs_dim=1):
@@ -30,137 +31,204 @@
     return lax.broadcasted_iota(jnp.int32, shape, len(shape) - 1)
 
 
-def arrange_kernel(slots_ref, r_ref, out_ref):
-    group = pl.program_id(0)
-    rows = r_ref.shape[0]
-    low = lanes((rows, WIDTH)) < BLOCK
-    for pair in range(out_ref.shape[2] // WIDTH):
-        halves = []
-        for side in range(2):
-            block = slots_ref[group * (out_ref.shape[2] // BLOCK) + 2 * pair + side]
-            tile = r_ref[:, pl.ds(pl.multiple_of((block // 2) * WIDTH, WIDTH), WIDTH)]
-            halves.append(pltpu.roll(tile, ((block + side) % 2) * BLOCK, 1))
-        out_ref[0, :, pair * WIDTH : (pair + 1) * WIDTH] = jnp.where(low, halves[0], halves[1])
-
-
-def arrange(r_factor, block_slots, groups):
-    rows, cols = r_factor.shape
-    return pl.pallas_call(
-        arrange_kernel,
-        out_shape=jax.ShapeDtypeStruct((groups, rows, cols // groups), jnp.float32),
-        grid_spec=pltpu.PrefetchScalarGridSpec(
-            num_scalar_prefetch=1,
-            grid=(groups,),
-            in_specs=[pl.BlockSpec((rows, cols), lambda g, s: (0, 0))],
-            out_specs=pl.BlockSpec((1, rows, cols // groups), lambda g, s: (g, 0, 0)),
-        ),
-    )(block_slots, r_factor)
-
-
-def gram_kernel(
-    zs, x_ref, out_ref, part, half_in, mine, z_in, full,
-    half_send, half_recv, rs_send, rs_recv, ag_send, ag_recv,
+def spread_kernel(
+    count, zs, slots_ref, r_ref, x_ref, g_ref,
+    blocks, stage, held, part, half_in, mine, z_in, full,
+    out_send, out_recv, half_send, half_recv, rs_send, rs_recv, ag_send, ag_recv, save_sem,
 ):
+    me = lax.axis_index("pair")
     row = lax.axis_index("row")
     z, core = row // 2, row % 2
     other = z * 2 + (1 - core)
-    half = mine.shape[0]
+    rows = r_ref.shape[0]
+    steps = held.shape[0]
+    half = mine.shape[1]
     chunk = half // zs
-
-    def peer(k):
-        return lax.rem(z + k, zs)
+    low = lanes((rows, WIDTH)) < BLOCK
+
+    def target(k):
+        return lax.rem(me + k, count)
+
+    def z_row(k):
+        return lax.rem(z + k, zs) * 2 + core
 
     barrier = pltpu.get_barrier_semaphore()
     pl.semaphore_signal(barrier, inc=1, device_id={"row": other}, device_id_type=MESH)
     for k in range(1, zs):
-        pl.semaphore_signal(
-            barrier, inc=1, device_id={"row": peer(k) * 2 + core}, device_id_type=MESH
-        )
-
-    def gram(side):
-        for i in range(half // WIDTH):
-            at = pl.multiple_of(side * half + i * WIDTH, WIDTH)
-            cols = x_ref[:, pl.ds(at, WIDTH)]
-            part[pl.ds(at, WIDTH), :] = mm(cols, cols, 0)
-
-    gram(1 - core)
-    pl.semaphore_wait(barrier, zs)
-    swap = pltpu.make_async_remote_copy(
-        src_ref=part.at[pl.ds(pl.multiple_of((1 - core) * half, half), half)],
-        dst_ref=half_in,
-        send_sem=half_send,
-        recv_sem=half_recv,
-        device_id={"row": other},
-        device_id_type=MESH,
-    )
-    swap.start()
-    gram(core)
-    swap.wait()
-    mine[...] = part[pl.ds(pl.multiple_of(core * half, half), half), :] + half_in[...]
-
-    def scatter(k):
+        pl.semaphore_signal(barrier, inc=1, device_id={"row": z_row(k)}, device_id_type=MESH)
+
+    def greet(k, carry):
+        pl.semaphore_signal(barrier, inc=1, device_id={"pair": target(k)}, device_id_type=MESH)
+        return carry
+
+    lax.fori_loop(1, count, greet, 0)
+
+    def lift(t, carry):
+        tile = r_ref[:, pl.ds(pl.multiple_of(t * WIDTH, WIDTH), WIDTH)]
+        blocks[2 * t] = tile
+        blocks[2 * t + 1] = pltpu.roll(tile, BLOCK, 1)
+        return carry
+
+    lax.fori_loop(0, blocks.shape[0] // 2, lift, 0, unroll=8)
+
+    def piece(group, s, i):
+        slot = group * 8 + 2 * (2 * i + s)
+        upper = blocks[slots_ref[slot]]
+        lower = blocks[slots_ref[slot + 1]]
+        return jnp.where(low, upper, pltpu.roll(lower, BLOCK, 1))
+
+    def arrange(s):
+        def body(k, carry):
+            group = target(k)
+            for i in range(2):
+                stage[s, group, :, i * WIDTH : (i + 1) * WIDTH] = piece(group, s, i)
+            return carry
+
+        return body
+
+    here = pl.ds(pl.multiple_of(me * rows, rows), rows)
+
+    def send(s, k):
         return pltpu.make_async_remote_copy(
-            src_ref=mine.at[pl.ds(pl.multiple_of(peer(k) * chunk, chunk), chunk)],
-            dst_ref=z_in.at[zs - k],
-            send_sem=rs_send.at[k],
-            recv_sem=rs_recv.at[zs - k],
-            device_id={"row": peer(k) * 2 + core},
+            src_ref=stage.at[s, target(k)],
+            dst_ref=held.at[s, here],
+            send_sem=out_send.at[s, k],
+            recv_sem=out_recv.at[s, count - k],
+            device_id={"pair": target(k)},
             device_id_type=MESH,
         )
 
-    for k in range(1, zs):
-        scatter(k).start()
+    def start(s):
+        def body(k, carry):
+            send(s, k).start()
+            return carry
+
+        return body
+
+    def both(s):
+        def body(k, carry):
+            arrange(s)(k, carry)
+            send(s, k).start()
+            return carry
+
+        return body
+
+    def finish(s):
+        def body(k, carry):
+            send(s, k).wait()
+            return carry
+
+        return body
+
+    lax.fori_loop(1, EARLY, arrange(0), 0)
+    pl.semaphore_wait(barrier, count + zs - 1)
+    lax.fori_loop(1, EARLY, start(0), 0)
+    lax.fori_loop(EARLY, count, both(0), 0)
+    for s in range(1, steps):
+        lax.fori_loop(1, count, both(s), 0)
+    for s in range(steps):
+        for i in range(2):
+            held[s, here, i * WIDTH : (i + 1) * WIDTH] = piece(me, s, i)
+
+    def gram(s, i):
+        cols = held[s, :, pl.ds(pl.multiple_of(i * WIDTH, WIDTH), WIDTH)]
+        part[s, pl.ds(pl.multiple_of(i * WIDTH, WIDTH), WIDTH), :] = mm(cols, cols, 0)
+
     own = pl.ds(pl.multiple_of(z * chunk, chunk), chunk)
-    for k in range(1, zs):
-        scatter(k).wait()
-    total = mine[own, :]
-    for k in range(1, zs):
-        total = total + z_in[k]
-    full[own, :] = total
-
-    def gather(k):
-        return pltpu.make_async_remote_copy(
-            src_ref=full.at[own],
-            dst_ref=full.at[own],
-            send_sem=ag_send.at[k],
-            recv_sem=ag_recv.at[zs - k],
-            device_id={"row": peer(k) * 2 + core},
+    for s in range(steps):
+        lax.fori_loop(1, count, finish(s), 0)
+        save = pltpu.make_async_copy(held.at[s], x_ref.at[s], save_sem.at[s])
+        save.start()
+        gram(s, 1 - core)
+        swap = pltpu.make_async_remote_copy(
+            src_ref=part.at[s, pl.ds(pl.multiple_of((1 - core) * half, half), half)],
+            dst_ref=half_in.at[s],
+            send_sem=half_send.at[s],
+            recv_sem=half_recv.at[s],
+            device_id={"row": other},
             device_id_type=MESH,
         )
-
-    for k in range(1, zs):
-        gather(k).start()
-    for k in range(1, zs):
-        gather(k).wait()
-    out_ref[...] = full[...]
-
-
-def half_grams(column):
-    rows, cols = column.shape
-    half = cols // 2
+        swap.start()
+        gram(s, core)
+        swap.wait()
+        mine[s] = part[s, pl.ds(pl.multiple_of(core * half, half), half), :] + half_in[s]
+
+        def scatter(k, s=s):
+            at = pl.multiple_of(lax.rem(z + k, zs) * chunk, chunk)
+            return pltpu.make_async_remote_copy(
+                src_ref=mine.at[s, pl.ds(at, chunk)],
+                dst_ref=z_in.at[s, zs - k],
+                send_sem=rs_send.at[s, k],
+                recv_sem=rs_recv.at[s, zs - k],
+                device_id={"row": z_row(k)},
+                device_id_type=MESH,
+            )
+
+        for k in range(1, zs):
+            scatter(k).start()
+        for k in range(1, zs):
+            scatter(k).wait()
+        total = mine[s, own, :]
+        for k in range(1, zs):
+            total = total + z_in[s, k]
+        full[s, own, :] = total
+
+        def gather(k, s=s):
+            return pltpu.make_async_remote_copy(
+                src_ref=full.at[s, own],
+                dst_ref=full.at[s, own],
+                send_sem=ag_send.at[s, k],
+                recv_sem=ag_recv.at[s, zs - k],
+                device_id={"row": z_row(k)},
+                device_id_type=MESH,
+            )
+
+        for k in range(1, zs):
+            gather(k).start()
+        for k in range(1, zs):
+            gather(k).wait()
+        g_ref[s * half : (s + 1) * half, :] = full[s]
+        save.wait()
+
+
+def spread(r_factor, block_slots):
+    rows, cols = r_factor.shape
+    count = lax.axis_size("pair")
     zs = lax.axis_size("row") // 2
+    steps = 2
+    wide = cols // count // steps
+    half = WIDTH
     vmem = pl.BlockSpec(memory_space=pltpu.VMEM)
     dma = pltpu.SemaphoreType.DMA
     return pl.pallas_call(
-        functools.partial(gram_kernel, zs),
-        out_shape=jax.ShapeDtypeStruct((half, WIDTH), jnp.float32),
-        in_specs=[vmem],
-        out_specs=vmem,
+        functools.partial(spread_kernel, count, zs),
+        out_shape=(
+            jax.ShapeDtypeStruct((steps, rows * count, wide), jnp.float32),
+            jax.ShapeDtypeStruct((steps * half, WIDTH), jnp.float32),
+        ),
+        in_specs=[pl.BlockSpec(memory_space=pltpu.SMEM), vmem],
+        out_specs=(pl.BlockSpec(memory_space=pl.ANY), vmem),
         scratch_shapes=[
-            pltpu.VMEM((cols, WIDTH), jnp.float32),
-            pltpu.VMEM((half, WIDTH), jnp.float32),
-            pltpu.VMEM((half, WIDTH), jnp.float32),
-            pltpu.VMEM((zs, half // zs, WIDTH), jnp.float32),
-            pltpu.VMEM((half, WIDTH), jnp.float32),
-            dma,
-            dma,
-            dma((zs,)),
-            dma((zs,)),
-            dma((zs,)),
-            dma((zs,)),
+            pltpu.VMEM((cols // BLOCK, rows, WIDTH), jnp.float32),
+            pltpu.VMEM((steps, count, rows, wide), jnp.float32),
+            pltpu.VMEM((steps, rows * count, wide), jnp.float32),
+            pltpu.VMEM((steps, 2 * half, WIDTH), jnp.float32),
+            pltpu.VMEM((steps, half, WIDTH), jnp.float32),
+            pltpu.VMEM((steps, half, WIDTH), jnp.float32),
+            pltpu.VMEM((steps, zs, half // zs, WIDTH), jnp.float32),
+            pltpu.VMEM((steps, half, WIDTH), jnp.float32),
+            dma((steps, count)),
+            dma((steps, count)),
+            dma((steps,)),
+            dma((steps,)),
+            dma((steps, zs)),
+            dma((steps, zs)),
+            dma((steps, zs)),
+            dma((steps, zs)),
+            dma((steps,)),
         ],
         compiler_params=pltpu.CompilerParams(collective_id=0, has_side_effects=True),
-    )(column)
+    )(block_slots, r_factor)
 
 
 def rotation_kernel(g_ref, out_ref, gram, basis, power, turn):
@@ -231,17 +299,19 @@
 
 
 def apply_kernel(
-    xs, ys, x_ref, v_ref, out_ref, ratio_ref,
-    v_in, turned, packed, landed, sum_x, sum_y,
-    v_send, v_recv, edge_send, edge_recv, x_send, x_recv, y_send, y_recv,
+    xs, ys, x_hbm, v_ref, out_ref, ratio_ref,
+    x_ref, v_in, turned, packed, landed, sum_x, sum_y,
+    x_sem, v_send, v_recv, edge_send, edge_recv, x_send, x_recv, y_send, y_recv,
 ):
+    load = pltpu.make_async_copy(x_hbm, x_ref, x_sem)
+    load.start()
     pair = lax.axis_index("pair")
     row = lax.axis_index("row")
     core = row % 2
     other = (row // 2) * 2 + (1 - core)
     count = xs * ys
     y, x = pair // xs, pair % xs
-    rows = x_ref.shape[0]
+    rows = x_ref.shape[1]
     half = rows // 2
     vrows = v_ref.shape[0] - 8
 
@@ -260,7 +330,8 @@
 
     def turn(source, j, local):
         v = source[pl.ds(pl.multiple_of(local * WIDTH, WIDTH), WIDTH), :]
-        turned[j] = mm(x_ref[:, pl.ds(pl.multiple_of(j * WIDTH, WIDTH), WIDTH)], v)
+        at = pl.multiple_of((j // 2) * WIDTH, WIDTH)
+        turned[j] = mm(x_ref[j % 2, :, pl.ds(at, WIDTH)], v)
 
     lane = lanes((half, WIDTH))
 
@@ -280,6 +351,7 @@
         )
 
     away = 1 - core
+    load.wait()
     turn(v_ref, 3 * core, core)
     edge(core)
     pl.semaphore_wait(barrier, len(peers) + 1)
@@ -360,7 +432,8 @@
 
 
 def apply_and_move(column, turns):
-    rows, cols = column.shape
+    steps, rows, wide = column.shape
+    cols = steps * wide
     count = lax.axis_size("pair")
     xs = X_CHIPS
     ys = count // xs
@@ -372,15 +445,17 @@
             jax.ShapeDtypeStruct((rows, cols), jnp.float32),
             jax.ShapeDtypeStruct((8, WIDTH), jnp.float32),
         ),
-        in_specs=[vmem, vmem],
+        in_specs=[pl.BlockSpec(memory_space=pl.ANY), vmem],
         out_specs=(vmem, vmem),
         scratch_shapes=[
+            pltpu.VMEM(column.shape, jnp.float32),
             pltpu.VMEM(turns.shape, jnp.float32),
             pltpu.VMEM((cols // WIDTH, rows, WIDTH), jnp.float32),
             pltpu.VMEM((2, rows // 2, WIDTH), jnp.float32),
             pltpu.VMEM((2, rows // 2, WIDTH), jnp.float32),
             pltpu.VMEM((xs, 8, WIDTH), jnp.float32),
             pltpu.VMEM((ys, 8, WIDTH), jnp.float32),
+            dma,
             dma,
             dma,
             dma((2,)),
@@ -395,13 +470,8 @@
 
 
 def on_device(r_factor, block_slots):
-    rows_in, total_cols = r_factor.shape
-    count = lax.axis_size("pair")
-    slabs = arrange(r_factor, block_slots, count)
-    received = lax.all_to_all(slabs, "pair", split_axis=0, concat_axis=0, tiled=True)
-    column = received.reshape(rows_in * count, total_cols // count)
-    turns = rotations(half_grams(column))
-    rotated, ratio = apply_and_move(column, turns)
+    column, grams = spread(r_factor, block_slots)
+    rotated, ratio = apply_and_move(column, rotations(grams))
     return (rotated, ratio[0, 0])
 
 

time: 135 us -> 111 us (0.82)
  blocking collectives: 59.3 us -> 0 us
  Pallas kernels: 70 us -> 106 us
    all_to_all x1 -> x0, blocking collectives: 59.3 us -> none  [on_device(): lax.all_to_all(slabs, 'pair', split_axis=0, concat_axis=0, tiled=True)]
    pallas_call x2 -> x1, Pallas kernels: 40.6 us -> 76.5 us  [spread(): pl.pallas_call(functools.partial(spread_kernel, count, zs), out_shape=(ja...]
where the time goes in v2:
time: 111 us
  Pallas kernels  106 us (95%)
  local copies, waits for them, and re-layouts  4.26 us (4%)
    pallas_call x1, Pallas kernels, spread(): pl.pallas_call(functools.partial(spread_kernel, count, zs), out_shape=(ja...  76.5 us
    pallas_call x1, Pallas kernels, apply_and_move(): pl.pallas_call(functools.partial(apply_kernel, xs, ys), out_shape=(jax.Sh...  22.9 us
    pallas_call x1, Pallas kernels, rotations(): pl.pallas_call(rotation_kernel, out_shape=jax.ShapeDtypeStruct((grams.sha...  6.87 us
    unnamed x1, local copies, waits for them, and re-layouts  3.08 us

profile of v2, /device:TPU:1, one launch (start us, length us, event | category | flops | bytes accessed | tf_op | source)
XLA Modules:
  0.0 111.1 jit_solution(10430609509324316529)
XLA Ops:
  0.6 76.5 %shard_map.41 = (f32[2,1024,256]{2,1,0:T(8,128)}, f32[256,128]{1,0:T(8,128)}) custom-call(s32[256]{0:T(256)} %slots_ref.1, f32[32,16384]{1,0:T(8,128)} %r_ref.1), custom_call_target="tpu_custom_call" | custom-call | tf_op jit(solution)/shard_map/pallas_call | solution.py:203
  77.1 6.9 %shard_map.42.v_ref = f32[264,128]{1,0:T(8,128)} custom-call(f32[256,128]{1,0:T(8,128)} %get-tuple-element.7.g_ref), custom_call_target="tpu_custom_call" | custom-call | tf_op jit(solution)/shard_map/pallas_call | solution.py:292
  84.0 22.9 %shard_map.43 = (f32[1024,512]{1,0:T(8,128)}, f32[8,128]{1,0:T(8,128)}) custom-call(f32[2,1024,256]{2,1,0:T(8,128)} %get-tuple-element.6.x_hbm, f32[264,128]{1,0:T(8,128)} %shard_map.42.v_ref), custom_call_target="tpu_custom_call" | custom-call | tf_op jit(solution)/shard_map/pallas_call | solution.py:442
  106.9 1.2 %slice.3 = f32[1,1]{1,0:T(1,128)} slice(f32[8,128]{1,0:T(8,128)} %get-tuple-element.9), slice={[0:1], [0:1]} | slice | bytes 8 | tf_op jit(solution)/shard_map/slice | solution.py:475
  108.1 3.1 %copy.5 = f32[1024,512]{1,0:T(8,128)} copy(f32[1024,512]{1,0:T(8,128)} %get-tuple-element.12) | data formatting | bytes 4194304

commit v3 on v2

--- a/solution.py
+++ b/solution.py
@@ -15,6 +15,7 @@
 NEUMANN_TOL = 1e-8
 X_CHIPS = 4
 EARLY = 8
+PLACE_STEPS = 4
 
 
 def mm(lhs, rhs, lhs_dim=1):
@@ -32,10 +33,12 @@
 
 
 def spread_kernel(
-    count, zs, slots_ref, r_ref, x_ref, g_ref,
-    blocks, stage, held, part, half_in, mine, z_in, full,
-    out_send, out_recv, half_send, half_recv, rs_send, rs_recv, ag_send, ag_recv, save_sem,
+    count, zs, slots_ref, r_hbm, x_ref, g_ref,
+    r_ref, blocks, stage, held, part, half_in, mine, z_in, full,
+    out_send, out_recv, half_send, half_recv, rs_send, rs_recv, ag_send, ag_recv, save_sem, load_sem,
 ):
+    load = pltpu.make_async_copy(r_hbm, r_ref, load_sem)
+    load.start()
     me = lax.axis_index("pair")
     row = lax.axis_index("row")
     z, core = row // 2, row % 2
@@ -69,6 +72,7 @@
         blocks[2 * t + 1] = pltpu.roll(tile, BLOCK, 1)
         return carry
 
+    load.wait()
     lax.fori_loop(0, blocks.shape[0] // 2, lift, 0, unroll=8)
 
     def piece(group, s, i):
@@ -206,9 +210,10 @@
             jax.ShapeDtypeStruct((steps, rows * count, wide), jnp.float32),
             jax.ShapeDtypeStruct((steps * half, WIDTH), jnp.float32),
         ),
-        in_specs=[pl.BlockSpec(memory_space=pltpu.SMEM), vmem],
+        in_specs=[pl.BlockSpec(memory_space=pltpu.SMEM), pl.BlockSpec(memory_space=pl.ANY)],
         out_specs=(pl.BlockSpec(memory_space=pl.ANY), vmem),
         scratch_shapes=[
+            pltpu.VMEM((rows, cols), jnp.float32),
             pltpu.VMEM((cols // BLOCK, rows, WIDTH), jnp.float32),
             pltpu.VMEM((steps, count, rows, wide), jnp.float32),
             pltpu.VMEM((steps, rows * count, wide), jnp.float32),
@@ -226,13 +231,15 @@
             dma((steps, zs)),
             dma((steps, zs)),
             dma((steps,)),
+            dma,
         ],
         compiler_params=pltpu.CompilerParams(collective_id=0, has_side_effects=True),
     )(block_slots, r_factor)
 
 
-def rotation_kernel(g_ref, out_ref, gram, basis, power, turn):
-    pairs = gram.shape[0]
+def rotation_kernel(g_ref, out_ref, tall, state):
+    pairs = tall.shape[0]
+    top, bottom = slice(0, WIDTH), slice(WIDTH, 2 * WIDTH)
     row_ids = lax.broadcasted_iota(jnp.int32, (WIDTH, WIDTH), 0)
     unit = row_ids == lanes((WIDTH, WIDTH))
     eye = jnp.where(unit, 1.0, 0.0).astype(jnp.float32)
@@ -240,7 +247,7 @@
     on = jnp.zeros((1, WIDTH), jnp.float32)
     for p in range(pairs):
         value = g_ref[p * WIDTH : (p + 1) * WIDTH, :]
-        gram[p] = value
+        tall[p, top, :] = value
         squares = value * value
         off = off + jnp.sum(jnp.where(unit, 0.0, squares), axis=0, keepdims=True)
         on = on + jnp.sum(jnp.where(unit, squares, 0.0), axis=0, keepdims=True)
@@ -252,7 +259,7 @@
     for sweep in range(ITERS):
         ratio = jnp.zeros((), jnp.float32)
         for p in range(pairs):
-            value = gram[p]
+            value = tall[p, top, :]
             on_diag = jnp.where(unit, value, 0.0)
             d_col = jnp.sum(on_diag, axis=1, keepdims=True)
             d_row = jnp.sum(on_diag, axis=0, keepdims=True)
@@ -260,48 +267,48 @@
             square = mm(skew, skew)
             bound = jnp.max(jnp.sum(jnp.abs(square), axis=0, keepdims=True))
             scale = 2.0 / (2.0 + bound)
-            power[p] = eye - scale * (eye - square)
-            turn[p] = scale * (eye - 2.0 * skew + square)
+            state[p, top, :] = scale * (eye - 2.0 * skew + square)
+            state[p, bottom, :] = eye - scale * (eye - square)
             ratio = jnp.maximum(ratio, bound / (2.0 + bound))
 
         def step(carry):
             for p in range(pairs):
-                e = power[p]
-                v = turn[p]
-                turn[p] = v + mm(v, e)
-                power[p] = mm(e, e)
+                both = mm(state[p], state[p, bottom, :])
+                state[p, top, :] = state[p, top, :] + both[top]
+                state[p, bottom, :] = both[bottom]
             return carry * carry
 
         lax.while_loop(lambda left: left > NEUMANN_TOL, step, ratio)
         for p in range(pairs):
-            v = turn[p]
-            if sweep + 1 < ITERS:
-                gram[p] = mm(v, mm(gram[p], v), 0)
+            v = state[p, top, :]
             if sweep == 0:
-                basis[p] = v
+                tall[p, top, :] = mm(v, mm(tall[p, top, :], v), 0)
+                tall[p, bottom, :] = v
             elif sweep + 1 < ITERS:
-                basis[p] = mm(basis[p], v)
+                both = mm(tall[p], v)
+                tall[p, top, :] = mm(v, both[top], 0)
+                tall[p, bottom, :] = both[bottom]
             else:
-                out_ref[p * WIDTH : (p + 1) * WIDTH, :] = mm(basis[p], v)
+                out_ref[p * WIDTH : (p + 1) * WIDTH, :] = mm(tall[p, bottom, :], v)
 
 
 def rotations(grams):
     vmem = pl.BlockSpec(memory_space=pltpu.VMEM)
     pairs = grams.shape[0] // WIDTH
-    work = pltpu.VMEM((pairs, WIDTH, WIDTH), jnp.float32)
+    work = pltpu.VMEM((pairs, 2 * WIDTH, WIDTH), jnp.float32)
     return pl.pallas_call(
         rotation_kernel,
         out_shape=jax.ShapeDtypeStruct((grams.shape[0] + 8, WIDTH), jnp.float32),
         in_specs=[vmem],
         out_specs=vmem,
-        scratch_shapes=[work] * 4,
+        scratch_shapes=[work] * 2,
     )(grams)
 
 
 def apply_kernel(
-    xs, ys, x_hbm, v_ref, out_ref, ratio_ref,
-    x_ref, v_in, turned, packed, landed, sum_x, sum_y,
-    x_sem, v_send, v_recv, edge_send, edge_recv, x_send, x_recv, y_send, y_recv,
+    xs, ys, x_hbm, v_ref, turned_hbm, landed, ratio_ref,
+    x_ref, v_in, turned, packed, sum_x, sum_y,
+    x_sem, save_sem, v_send, v_recv, edge_send, edge_recv, x_send, x_recv, y_send, y_recv,
 ):
     load = pltpu.make_async_copy(x_hbm, x_ref, x_sem)
     load.start()
@@ -313,7 +320,7 @@
     y, x = pair // xs, pair % xs
     rows = x_ref.shape[1]
     half = rows // 2
-    vrows = v_ref.shape[0] - 8
+    vrows = v_in.shape[0]
 
     def x_peer(k):
         return y * xs + lax.rem(x + k, xs)
@@ -323,15 +330,23 @@
 
     right, left = lax.rem(pair + 1, count), lax.rem(pair + count - 1, count)
     barrier = pltpu.get_barrier_semaphore()
-    pl.semaphore_signal(barrier, inc=1, device_id={"row": other}, device_id_type=MESH)
-    peers = [left, right] + [x_peer(k) for k in range(1, xs)] + [y_peer(k) for k in range(1, ys)]
+    peers = [(y_peer(k), row) for k in range(1, ys)]
+    peers += [(left, row), (right, row)]
+    peers += [(x_peer(k), row) for k in range(1, xs)]
+    peers += [(x_peer(k), other) for k in range(xs)]
     for peer in peers:
-        pl.semaphore_signal(barrier, inc=1, device_id={"pair": peer}, device_id_type=MESH)
+        pl.semaphore_signal(
+            barrier, inc=1, device_id={"pair": peer[0], "row": peer[1]}, device_id_type=MESH
+        )
+    sum_x[core, x] = v_ref[vrows : vrows + 8, :]
 
     def turn(source, j, local):
         v = source[pl.ds(pl.multiple_of(local * WIDTH, WIDTH), WIDTH), :]
         at = pl.multiple_of((j // 2) * WIDTH, WIDTH)
         turned[j] = mm(x_ref[j % 2, :, pl.ds(at, WIDTH)], v)
+
+    def save(j):
+        return pltpu.make_async_copy(turned.at[j], turned_hbm.at[j], save_sem.at[j])
 
     lane = lanes((half, WIDTH))
 
@@ -350,13 +365,25 @@
             device_id_type=MESH,
         )
 
+    def x_copy(k, crossed):
+        return pltpu.make_async_remote_copy(
+            src_ref=sum_x.at[core, x],
+            dst_ref=sum_x.at[core, x],
+            send_sem=x_send.at[crossed, k],
+            recv_sem=x_recv.at[crossed, (xs - k) % xs],
+            device_id={"pair": x_peer(k), "row": other if crossed else row},
+            device_id_type=MESH,
+        )
+
+    x_copies = [x_copy(k, crossed) for crossed in range(2) for k in range(1 - crossed, xs)]
+
     away = 1 - core
     load.wait()
     turn(v_ref, 3 * core, core)
     edge(core)
-    pl.semaphore_wait(barrier, len(peers) + 1)
+    pl.semaphore_wait(barrier, len(peers))
     swap = pltpu.make_async_remote_copy(
-        src_ref=v_ref,
+        src_ref=v_ref.at[0:vrows],
         dst_ref=v_in,
         send_sem=v_send,
         recv_sem=v_recv,
@@ -364,33 +391,22 @@
         device_id_type=MESH,
     )
     swap.start()
+    for copy in x_copies:
+        copy.start()
     edge_copy(core).start()
+    save(3 * core).start()
     turn(v_ref, 1 + core, away)
+    save(1 + core).start()
     swap.wait()
     turn(v_in, 3 * away, away)
     edge(away)
     edge_copy(away).start()
 
-    sum_x[x] = v_ref[vrows : vrows + 8, :] + v_in[vrows : vrows + 8, :]
-
-    def x_copy(k):
-        return pltpu.make_async_remote_copy(
-            src_ref=sum_x.at[x],
-            dst_ref=sum_x.at[x],
-            send_sem=x_send.at[k],
-            recv_sem=x_recv.at[xs - k],
-            device_id={"pair": x_peer(k)},
-            device_id_type=MESH,
-        )
-
-    for k in range(1, xs):
-        x_copy(k).start()
-    turn(v_in, 2 - core, core)
-    for k in range(1, xs):
-        x_copy(k).wait()
-    total = sum_x[0]
-    for k in range(1, xs):
-        total = total + sum_x[k]
+    for copy in x_copies:
+        copy.wait()
+    total = jnp.zeros((8, WIDTH), jnp.float32)
+    for k in range(xs):
+        total = total + (sum_x[0, k] + sum_x[1, k])
     sum_y[y] = total
 
     def y_copy(k):
@@ -405,13 +421,9 @@
 
     for k in range(1, ys):
         y_copy(k).start()
-
-    low = lanes((rows, WIDTH)) < BLOCK
-    first, last = pair == 0, pair == count - 1
-    out_ref[:, 2 * WIDTH : 3 * WIDTH] = jnp.where(low, turned[1], turned[3])
-    upper = jnp.where(first, pltpu.roll(turned[0], BLOCK, 1), turned[0])
-    out_ref[:, WIDTH : 2 * WIDTH] = jnp.where(low, upper, turned[2])
-
+    save(3 * away).start()
+    turn(v_in, 2 - core, core)
+    save(2 - core).start()
     for k in range(1, ys):
         y_copy(k).wait()
     total = sum_y[0]
@@ -420,48 +432,45 @@
     off = jnp.sum(total[0:1, :], axis=1, keepdims=True)
     on = jnp.sum(total[1:2, :], axis=1, keepdims=True)
     ratio_ref[...] = jnp.broadcast_to(jnp.sqrt(off / on), ratio_ref.shape)
-
+    for j in range(turned.shape[0]):
+        save(j).wait()
     edge_copy(core).wait()
     edge_copy(away).wait()
-    down = jnp.concatenate([landed[0], pltpu.roll(landed[0], BLOCK, 1)], axis=0)
-    down = jnp.where(last, pltpu.roll(turned[3], BLOCK, 1), down)
-    out_ref[:, 3 * WIDTH : 4 * WIDTH] = jnp.where(low, turned[2], down)
-    up = jnp.concatenate([landed[1], pltpu.roll(landed[1], BLOCK, 1)], axis=0)
-    up = jnp.where(first, turned[0], up)
-    out_ref[:, 0:WIDTH] = jnp.where(low, up, turned[1])
 
 
 def apply_and_move(column, turns):
     steps, rows, wide = column.shape
-    cols = steps * wide
+    pairs = steps * wide // WIDTH
     count = lax.axis_size("pair")
     xs = X_CHIPS
     ys = count // xs
     vmem = pl.BlockSpec(memory_space=pltpu.VMEM)
+    hbm = pl.BlockSpec(memory_space=pl.ANY)
     dma = pltpu.SemaphoreType.DMA
     return pl.pallas_call(
         functools.partial(apply_kernel, xs, ys),
         out_shape=(
-            jax.ShapeDtypeStruct((rows, cols), jnp.float32),
+            jax.ShapeDtypeStruct((pairs, rows, WIDTH), jnp.float32),
+            jax.ShapeDtypeStruct((2, rows // 2, WIDTH), jnp.float32),
             jax.ShapeDtypeStruct((8, WIDTH), jnp.float32),
         ),
-        in_specs=[pl.BlockSpec(memory_space=pl.ANY), vmem],
-        out_specs=(vmem, vmem),
+        in_specs=[hbm, vmem],
+        out_specs=(hbm, hbm, vmem),
         scratch_shapes=[
             pltpu.VMEM(column.shape, jnp.float32),
-            pltpu.VMEM(turns.shape, jnp.float32),
-            pltpu.VMEM((cols // WIDTH, rows, WIDTH), jnp.float32),
+            pltpu.VMEM((turns.shape[0] - 8, WIDTH), jnp.float32),
+            pltpu.VMEM((pairs, rows, WIDTH), jnp.float32),
             pltpu.VMEM((2, rows // 2, WIDTH), jnp.float32),
-            pltpu.VMEM((2, rows // 2, WIDTH), jnp.float32),
-            pltpu.VMEM((xs, 8, WIDTH), jnp.float32),
+            pltpu.VMEM((2, xs, 8, WIDTH), jnp.float32),
             pltpu.VMEM((ys, 8, WIDTH), jnp.float32),
             dma,
+            dma((pairs,)),
             dma,
             dma,
             dma((2,)),
             dma((2,)),
-            dma((xs,)),
-            dma((xs,)),
+            dma((2, xs)),
+            dma((2, xs)),
             dma((ys,)),
             dma((ys,)),
         ],
@@ -469,10 +478,50 @@
     )(column, turns)
 
 
+def place_kernel(last_pair, turned, landed, ratio_in, out_ref, ratio_ref):
+    pair = lax.axis_index("pair")
+    first, last = pair == 0, pair == last_pair
+    swapped = pl.program_id(0) >= pl.num_programs(0) // 2
+    low = lanes(landed.shape[1:]) < BLOCK
+    from_right, from_left = landed[0], landed[1]
+    from_right = jnp.where(swapped, pltpu.roll(from_right, BLOCK, 1), from_right)
+    from_left = jnp.where(swapped, pltpu.roll(from_left, BLOCK, 1), from_left)
+    up = jnp.where(first, turned[0], from_left)
+    next_up = jnp.where(first, pltpu.roll(turned[0], BLOCK, 1), turned[0])
+    down = jnp.where(last, pltpu.roll(turned[3], BLOCK, 1), from_right)
+    out_ref[:, 0:WIDTH] = jnp.where(low, up, turned[1])
+    out_ref[:, WIDTH : 2 * WIDTH] = jnp.where(low, next_up, turned[2])
+    out_ref[:, 2 * WIDTH : 3 * WIDTH] = jnp.where(low, turned[1], turned[3])
+    out_ref[:, 3 * WIDTH : 4 * WIDTH] = jnp.where(low, turned[2], down)
+    ratio_ref[...] = ratio_in[0:1, 0:1]
+
+
+def place(turned, landed, ratio):
+    pairs, rows, _ = turned.shape
+    tile = rows // PLACE_STEPS
+    return pl.pallas_call(
+        functools.partial(place_kernel, lax.axis_size("pair") - 1),
+        out_shape=(
+            jax.ShapeDtypeStruct((rows, pairs * WIDTH), jnp.float32),
+            jax.ShapeDtypeStruct((1, 1), jnp.float32),
+        ),
+        grid=(PLACE_STEPS,),
+        in_specs=[
+            pl.BlockSpec((pairs, tile, WIDTH), lambda g: (0, g, 0)),
+            pl.BlockSpec((2, tile, WIDTH), lambda g: (0, lax.rem(g, PLACE_STEPS // 2), 0)),
+            pl.BlockSpec((8, WIDTH), lambda g: (0, 0)),
+        ],
+        out_specs=(
+            pl.BlockSpec((tile, pairs * WIDTH), lambda g: (g, 0)),
+            pl.BlockSpec((1, 1), lambda g: (0, 0)),
+        ),
+    )(turned, landed, ratio)
+
+
 def on_device(r_factor, block_slots):
     column, grams = spread(r_factor, block_slots)
-    rotated, ratio = apply_and_move(column, rotations(grams))
-    return (rotated, ratio[0, 0])
+    rotated, ratio = place(*apply_and_move(column, rotations(grams)))
+    return (rotated, ratio.reshape(()))
 
 
 def solution(mesh):

time: 111 us -> 107 us (0.964)
  local copies, waits for them, and re-layouts: 4.26 us -> 0 us
    pallas_call x1, Pallas kernels: 22.9 us -> 16.7 us  [apply_and_move(): pl.pallas_call(functools.partial(apply_kernel, xs, ys), out_shape=(jax.Sh...]
    pallas_call x0 -> x1, Pallas kernels: none -> 4.31 us  [place(): pl.pallas_call(functools.partial(place_kernel, lax.axis_size('pair') - 1)...]
    unnamed x1 -> x0, local copies, waits for them, and re-layouts: 3.08 us -> none
    slice x1 -> x0, local copies, waits for them, and re-layouts: 1.19 us -> none  [on_device(): return (rotated, ratio[0, 0])]
where the time goes in v3:
time: 107 us; the launch traced here: 106 us
  Pallas kernels  106 us (99%)
    pallas_call x1, Pallas kernels, spread(): pl.pallas_call(functools.partial(spread_kernel, count, zs), out_shape=(ja...  77.3 us
    pallas_call x1, Pallas kernels, apply_and_move(): pl.pallas_call(functools.partial(apply_kernel, xs, ys), out_shape=(jax.Sh...  16.7 us
    pallas_call x1, Pallas kernels, rotations(): pl.pallas_call(rotation_kernel, out_shape=jax.ShapeDtypeStruct((grams.sha...  7.45 us
    pallas_call x1, Pallas kernels, place(): pl.pallas_call(functools.partial(place_kernel, lax.axis_size('pair') - 1)...  4.31 us

profile of v3, /device:TPU:1, one launch (start us, length us, event | category | flops | bytes accessed | tf_op | source)
XLA Modules:
  0.0 106.4 jit_solution(11193616242806616307)
XLA Ops:
  0.6 77.3 %shard_map.41 = (f32[2,1024,256]{2,1,0:T(8,128)}, f32[256,128]{1,0:T(8,128)}) custom-call(s32[256]{0:T(256)} %slots_ref.1, f32[32,16384]{1,0:T(8,128)} %r_hbm.1), custom_call_target="tpu_custom_call" | custom-call | tf_op jit(solution)/shard_map/pallas_call | solution.py:207
  77.9 7.4 %shard_map.42.v_ref = f32[264,128]{1,0:T(8,128)} custom-call(f32[256,128]{1,0:T(8,128)} %get-tuple-element.10.g_ref), custom_call_target="tpu_custom_call" | custom-call | tf_op jit(solution)/shard_map/pallas_call | solution.py:299
  85.3 16.7 %shard_map.43 = (f32[4,1024,128]{2,1,0:T(8,128)}, f32[2,512,128]{2,1,0:T(8,128)}, f32[8,128]{1,0:T(8,128)}) custom-call(f32[2,1024,256]{2,1,0:T(8,128)} %get-tuple-element.9.x_hbm, f32[264,128]{1,0:T(8,128)} %shard_map.42.v_ref), custom_call_target="tpu_custom_call" | custom-call | tf_op jit(solution)/shard_map/pallas_call | solution.py:450
  102.1 4.3 %shard_map.44 = (f32[1024,512]{1,0:T(8,128)}, f32[1,1]{1,0:T(1,128)}) custom-call(f32[4,1024,128]{2,1,0:T(8,128)} %get-tuple-element.11.turned, f32[2,512,128]{2,1,0:T(8,128)} %get-tuple-element.12.landed, f32[8,128]{1,0:T(8,128)} %get-tuple-element.13.ratio_in), custom_call_target="tpu_custom_call" | custom-call | tf_op jit(solution)/shard_map/pallas_call | solution.py:502

commit v4 on v3

v4 whole, which is shorter than its diff:
```python
import functools

import jax
import jax.numpy as jnp
from jax import lax
from jax.experimental import pallas as pl
from jax.experimental.pallas import tpu as pltpu
from jax.sharding import PartitionSpec as P

BLOCK = 64
ITERS = 3
WIDTH = 2 * BLOCK
MESH = pl.DeviceIdType.MESH
HIGHEST = lax.Precision.HIGHEST
NEUMANN_TOL = 1e-8
X_CHIPS = 4
EARLY = 8
FACTORS = 12
PLACE_STEPS = 2


def mm(lhs, rhs, lhs_dim=1):
    return lax.dot_general(
        lhs,
        rhs,
        (((lhs_dim,), (0,)), ((), ())),
        precision=HIGHEST,
        preferred_element_type=jnp.float32,
    )


def lanes(shape):
    return lax.broadcasted_iota(jnp.int32, shape, len(shape) - 1)


def unit_mask():
    return lax.broadcasted_iota(jnp.int32, (WIDTH, WIDTH), 0) == lanes((WIDTH, WIDTH))


def skew_of(gram, unit):
    on_diag = jnp.where(unit, gram, 0.0)
    d_col = jnp.sum(on_diag, axis=1, keepdims=True)
    d_row = jnp.sum(on_diag, axis=0, keepdims=True)
    return gram * (d_col - d_row) / (2.0 * (d_col * d_col + d_row * d_row))


def series_start(state, skew, square, bound, unit):
    eye = jnp.where(unit, 1.0, 0.0).astype(jnp.float32)
    scale = 2.0 / (2.0 + bound)
    state[0:WIDTH, :] = scale * (eye - 2.0 * skew + square)
    state[WIDTH:, :] = eye - scale * (eye - square)


def series_step(state):
    both = mm(state[...], state[WIDTH:, :])
    state[0:WIDTH, :] = state[0:WIDTH, :] + both[0:WIDTH]
    state[WIDTH:, :] = both[WIDTH:]


def sweep_end(sweep, tall, state):
    v = state[0:WIDTH, :]
    if sweep == 0:
        tall[0:WIDTH, :] = mm(v, mm(tall[0:WIDTH, :], v), 0)
        tall[WIDTH:, :] = v
    elif sweep + 1 < ITERS:
        both = mm(tall[...], v)
        tall[0:WIDTH, :] = mm(v, both[0:WIDTH], 0)
        tall[WIDTH:, :] = both[WIDTH:]
    else:
        tall[WIDTH:, :] = mm(tall[WIDTH:, :], v)


def spread_kernel(
    xs, ys, zs, slots_ref, r_hbm, turned_hbm, landed, x_hbm, g_ref, ratio_ref,
    r_ref, blocks, stage, held, part, half_in, mine, z_in, full,
    tall, state, v_pair, turned, packed, sum_x, sum_y,
    out_send, out_recv, half_send, half_recv, rs_send, rs_recv, ag_send, ag_recv,
    load_sem, save_sem, v_send, v_recv, edge_send, edge_recv, g_send, g_recv,
    x_send, x_recv, y_send, y_recv,
):
    count = xs * ys
    load = pltpu.make_async_copy(r_hbm, r_ref, load_sem)
    load.start()
    me = lax.axis_index("pair")
    row = lax.axis_index("row")
    z, core = row // 2, row % 2
    other = z * 2 + (1 - core)
    rows = r_ref.shape[0]
    steps = held.shape[0]
    half = mine.shape[1]
    chunk = half // zs
    low = lanes((rows, WIDTH)) < BLOCK

    def target(k):
        return lax.rem(me + k, count)

    def z_row(k):
        return lax.rem(z + k, zs) * 2 + core

    barrier = pltpu.get_barrier_semaphore()
    y, x = me // xs, me % xs

    def x_peer(k):
        return y * xs + lax.rem(x + k, xs)

    def y_peer(k):
        return lax.rem(y + k, ys) * xs + x

    for k in range(xs):
        pl.semaphore_signal(
            barrier, inc=1, device_id={"pair": x_peer(k), "row": other}, device_id_type=MESH
        )
    for k in range(1, zs):
        pl.semaphore_signal(barrier, inc=1, device_id={"row": z_row(k)}, device_id_type=MESH)

    def greet(k, carry):
        pl.semaphore_signal(barrier, inc=1, device_id={"pair": target(k)}, device_id_type=MESH)
        return carry

    lax.fori_loop(1, count, greet, 0)

    def lift(t, carry):
        tile = r_ref[:, pl.ds(pl.multiple_of(t * WIDTH, WIDTH), WIDTH)]
        blocks[2 * t] = tile
        blocks[2 * t + 1] = pltpu.roll(tile, BLOCK, 1)
        return carry

    load.wait()
    lax.fori_loop(0, blocks.shape[0] // 2, lift, 0, unroll=8)

    def piece(group, s, i):
        slot = group * 8 + 2 * (1 + i if s else 3 * i)
        upper = blocks[slots_ref[slot]]
        lower = blocks[slots_ref[slot + 1]]
        return jnp.where(low, upper, pltpu.roll(lower, BLOCK, 1))

    def arrange(s):
        def body(k, carry):
            group = target(k)
            for i in range(2):
                stage[s, group, :, i * WIDTH : (i + 1) * WIDTH] = piece(group, s, i)
            return carry

        return body

    here = pl.ds(pl.multiple_of(me * rows, rows), rows)

    def send(s, k):
        return pltpu.make_async_remote_copy(
            src_ref=stage.at[s, target(k)],
            dst_ref=held.at[s, here],
            send_sem=out_send.at[s, k],
            recv_sem=out_recv.at[s, count - k],
            device_id={"pair": target(k)},
            device_id_type=MESH,
        )

    def start(s):
        def body(k, carry):
            send(s, k).start()
            return carry

        return body

    def both(s):
        def body(k, carry):
            arrange(s)(k, carry)
            send(s, k).start()
            return carry

        return body

    def finish(s):
        def body(k, carry):
            send(s, k).wait()
            return carry

        return body

    lax.fori_loop(1, EARLY, arrange(0), 0)
    pl.semaphore_wait(barrier, xs + zs - 1 + count - 1)
    lax.fori_loop(1, EARLY, start(0), 0)
    lax.fori_loop(EARLY, count, both(0), 0)
    for s in range(1, steps):
        lax.fori_loop(1, count, both(s), 0)
    for s in range(steps):
        for i in range(2):
            held[s, here, i * WIDTH : (i + 1) * WIDTH] = piece(me, s, i)

    def gram(s, i):
        cols = held[s, :, pl.ds(pl.multiple_of(i * WIDTH, WIDTH), WIDTH)]
        part[s, pl.ds(pl.multiple_of(i * WIDTH, WIDTH), WIDTH), :] = mm(cols, cols, 0)

    def save_turned(side):
        return pltpu.make_async_copy(turned.at[side], turned_hbm.at[side], save_sem.at[side])

    def edge_copy(side):
        return pltpu.make_async_remote_copy(
            src_ref=packed.at[side],
            dst_ref=landed.at[side],
            send_sem=edge_send.at[side],
            recv_sem=edge_recv.at[side],
            device_id={"pair": lax.rem(me + count + 2 * side - 1, count)},
            device_id_type=MESH,
        )

    unit = unit_mask()

    def rotate_edges():
        tall[0:WIDTH, :] = full[0]
        for sweep in range(ITERS):
            skew = skew_of(tall[0:WIDTH, :], unit)
            cells = jnp.sum(skew * skew, axis=0, keepdims=True)
            bound = 0.5 * jnp.sum(cells, axis=1, keepdims=True)
            series_start(state, skew, mm(skew, skew), bound, unit)

            def factor(k, carry):
                series_step(state)
                return carry

            lax.fori_loop(0, FACTORS, factor, 0)
            sweep_end(sweep, tall, state)
        v_pair[core] = tall[WIDTH:, :]
        swap = pltpu.make_async_remote_copy(
            src_ref=v_pair.at[core],
            dst_ref=v_pair.at[core],
            send_sem=v_send,
            recv_sem=v_recv,
            device_id={"row": other},
            device_id_type=MESH,
        )
        swap.start()
        swap.wait()
        edge_rows = turned.shape[1] // 2
        lane = lanes((edge_rows, WIDTH))
        for side in range(2):
            turned[side] = mm(held[0, :, side * WIDTH : (side + 1) * WIDTH], v_pair[side])
            save_turned(side).start()
            keep = (lane < BLOCK) == (side == 1)
            value = turned.at[side]
            rolled = pltpu.roll(value[edge_rows:, :], BLOCK, 1)
            packed[side] = jnp.where(keep, value[0:edge_rows, :], rolled)

    own = pl.ds(pl.multiple_of(z * chunk, chunk), chunk)
    for s in range(steps):
        lax.fori_loop(1, count, finish(s), 0)
        if s == 1:
            save = pltpu.make_async_copy(held.at[s], x_hbm, save_sem.at[2])
            save.start()
            for side in range(2):
                edge_copy(side).start()
        gram(s, 1 - core)
        swap = pltpu.make_async_remote_copy(
            src_ref=part.at[s, pl.ds(pl.multiple_of((1 - core) * half, half), half)],
            dst_ref=half_in.at[s],
            send_sem=half_send.at[s],
            recv_sem=half_recv.at[s],
            device_id={"row": other},
            device_id_type=MESH,
        )
        swap.start()
        gram(s, core)
        swap.wait()
        mine[s] = part[s, pl.ds(pl.multiple_of(core * half, half), half), :] + half_in[s]

        def scatter(k, s=s):
            at = pl.multiple_of(lax.rem(z + k, zs) * chunk, chunk)
            return pltpu.make_async_remote_copy(
                src_ref=mine.at[s, pl.ds(at, chunk)],
                dst_ref=z_in.at[s, zs - k],
                send_sem=rs_send.at[s, k],
                recv_sem=rs_recv.at[s, zs - k],
                device_id={"row": z_row(k)},
                device_id_type=MESH,
            )

        for k in range(1, zs):
            scatter(k).start()
        for k in range(1, zs):
            scatter(k).wait()
        total = mine[s, own, :]
        for k in range(1, zs):
            total = total + z_in[s, k]
        full[s, own, :] = total

        def gather(k, s=s):
            return pltpu.make_async_remote_copy(
                src_ref=full.at[s, own],
                dst_ref=full.at[s, own],
                send_sem=ag_send.at[s, k],
                recv_sem=ag_recv.at[s, zs - k],
                device_id={"row": z_row(k)},
                device_id_type=MESH,
            )

        for k in range(1, zs):
            gather(k).start()
        for k in range(1, zs):
            gather(k).wait()
        if s == 0:
            rotate_edges()

    pair_g = part.at[0]
    own_g = pl.ds(pl.multiple_of(core * half, half), half)
    pair_g[own_g, :] = full[1]
    g_swap = pltpu.make_async_remote_copy(
        src_ref=full.at[1],
        dst_ref=pair_g.at[own_g],
        send_sem=g_send,
        recv_sem=g_recv,
        device_id={"row": other},
        device_id_type=MESH,
    )

    off = jnp.zeros((1, WIDTH), jnp.float32)
    on = jnp.zeros((1, WIDTH), jnp.float32)
    for s in range(steps):
        squares = full[s] * full[s]
        off = off + jnp.sum(jnp.where(unit, 0.0, squares), axis=0, keepdims=True)
        on = on + jnp.sum(jnp.where(unit, squares, 0.0), axis=0, keepdims=True)
    tile_row = lax.broadcasted_iota(jnp.int32, (8, WIDTH), 0)
    sum_x[core, x] = jnp.where(tile_row == 0, off, jnp.where(tile_row == 1, on, 0.0))

    def x_copy(k, crossed):
        return pltpu.make_async_remote_copy(
            src_ref=sum_x.at[core, x],
            dst_ref=sum_x.at[core, x],
            send_sem=x_send.at[crossed, k],
            recv_sem=x_recv.at[crossed, (xs - k) % xs],
            device_id={"pair": x_peer(k), "row": other if crossed else row},
            device_id_type=MESH,
        )

    x_copies = [x_copy(k, crossed) for crossed in range(2) for k in range(1 - crossed, xs)]
    for copy in x_copies:
        copy.start()
    g_swap.start()
    for copy in x_copies:
        copy.wait()
    total = jnp.zeros((8, WIDTH), jnp.float32)
    for k in range(xs):
        total = total + (sum_x[0, k] + sum_x[1, k])
    sum_y[y] = total

    def y_copy(k):
        return pltpu.make_async_remote_copy(
            src_ref=sum_y.at[y],
            dst_ref=sum_y.at[y],
            send_sem=y_send.at[k],
            recv_sem=y_recv.at[ys - k],
            device_id={"pair": y_peer(k)},
            device_id_type=MESH,
        )

    for k in range(1, ys):
        y_copy(k).start()
    g_swap.wait()
    g_ref[...] = pair_g[...]
    for side in range(2):
        save_turned(side).wait()
        edge_copy(side).wait()
    save.wait()
    for k in range(1, ys):
        y_copy(k).wait()
    total = sum_y[0]
    for k in range(1, ys):
        total = total + sum_y[k]
    off = jnp.sum(total[0:1, :], axis=1, keepdims=True)
    on = jnp.sum(total[1:2, :], axis=1, keepdims=True)
    ratio_ref[...] = jnp.broadcast_to(jnp.sqrt(off / on), ratio_ref.shape)


def spread(r_factor, block_slots):
    rows, cols = r_factor.shape
    count = lax.axis_size("pair")
    xs = X_CHIPS
    ys = count // xs
    zs = lax.axis_size("row") // 2
    steps = 2
    wide = cols // count // steps
    tall_rows = rows * count
    half = WIDTH
    vmem = pl.BlockSpec(memory_space=pltpu.VMEM)
    hbm = pl.BlockSpec(memory_space=pl.ANY)
    dma = pltpu.SemaphoreType.DMA

    def f32(*shape):
        return jax.ShapeDtypeStruct(shape, jnp.float32)

    def work(*shape):
        return pltpu.VMEM(shape, jnp.float32)

    return pl.pallas_call(
        functools.partial(spread_kernel, xs, ys, zs),
        out_shape=(
            f32(2, tall_rows, WIDTH),
            f32(2, tall_rows // 2, WIDTH),
            f32(tall_rows, wide),
            f32(2 * half, WIDTH),
            f32(8, WIDTH),
        ),
        in_specs=[pl.BlockSpec(memory_space=pltpu.SMEM), hbm],
        out_specs=(hbm, hbm, hbm, vmem, vmem),
        scratch_shapes=[
            work(rows, cols),
            work(cols // BLOCK, rows, WIDTH),
            work(steps, count, rows, wide),
            work(steps, tall_rows, wide),
            work(steps, 2 * half, WIDTH),
            work(steps, half, WIDTH),
            work(steps, half, WIDTH),
            work(steps, zs, half // zs, WIDTH),
            work(steps, half, WIDTH),
            work(2 * WIDTH, WIDTH),
            work(2 * WIDTH, WIDTH),
            work(2, WIDTH, WIDTH),
            work(2, tall_rows, WIDTH),
            work(2, tall_rows // 2, WIDTH),
            work(2, xs, 8, WIDTH),
            work(ys, 8, WIDTH),
            dma((steps, count)),
            dma((steps, count)),
            dma((steps,)),
            dma((steps,)),
            dma((steps, zs)),
            dma((steps, zs)),
            dma((steps, zs)),
            dma((steps, zs)),
            dma,
            dma((3,)),
            dma,
            dma,
            dma((2,)),
            dma((2,)),
            dma,
            dma,
            dma((2, xs)),
            dma((2, xs)),
            dma((ys,)),
            dma((ys,)),
        ],
        compiler_params=pltpu.CompilerParams(collective_id=0, has_side_effects=True),
    )(block_slots, r_factor)


def rotation_kernel(g_ref, out_ref, tall, state):
    pairs = tall.shape[0]
    unit = unit_mask()
    for p in range(pairs):
        tall[p, 0:WIDTH, :] = g_ref[p * WIDTH : (p + 1) * WIDTH, :]
    for sweep in range(ITERS):
        ratio = jnp.zeros((), jnp.float32)
        for p in range(pairs):
            skew = skew_of(tall[p, 0:WIDTH, :], unit)
            square = mm(skew, skew)
            bound = jnp.max(jnp.sum(jnp.abs(square), axis=0, keepdims=True))
            series_start(state.at[p], skew, square, bound, unit)
            ratio = jnp.maximum(ratio, bound / (2.0 + bound))

        def step(carry):
            for p in range(pairs):
                series_step(state.at[p])
            return carry * carry

        lax.while_loop(lambda left: left > NEUMANN_TOL, step, ratio)
        for p in range(pairs):
            sweep_end(sweep, tall.at[p], state.at[p])
    for p in range(pairs):
        out_ref[p] = tall[p, WIDTH:, :]


def rotations(grams):
    vmem = pl.BlockSpec(memory_space=pltpu.VMEM)
    pairs = grams.shape[0] // WIDTH
    work = pltpu.VMEM((pairs, 2 * WIDTH, WIDTH), jnp.float32)
    return pl.pallas_call(
        rotation_kernel,
        out_shape=jax.ShapeDtypeStruct((pairs, WIDTH, WIDTH), jnp.float32),
        in_specs=[vmem],
        out_specs=vmem,
        scratch_shapes=[work] * 2,
    )(grams)


def place_kernel(last_pair, v_ref, x_ref, turned, landed, ratio_in, out_ref, ratio_ref):
    pair = lax.axis_index("pair")
    first, last = pair == 0, pair == last_pair
    swapped = pl.program_id(0) >= pl.num_programs(0) // 2
    low = lanes(landed.shape[1:]) < BLOCK
    from_right, from_left = landed[0], landed[1]
    from_right = jnp.where(swapped, pltpu.roll(from_right, BLOCK, 1), from_right)
    from_left = jnp.where(swapped, pltpu.roll(from_left, BLOCK, 1), from_left)
    second = mm(x_ref[:, 0:WIDTH], v_ref[0])
    third = mm(x_ref[:, WIDTH : 2 * WIDTH], v_ref[1])
    up = jnp.where(first, turned[0], from_left)
    next_up = jnp.where(first, pltpu.roll(turned[0], BLOCK, 1), turned[0])
    down = jnp.where(last, pltpu.roll(turned[1], BLOCK, 1), from_right)
    out_ref[:, 0:WIDTH] = jnp.where(low, up, second)
    out_ref[:, WIDTH : 2 * WIDTH] = jnp.where(low, next_up, third)
    out_ref[:, 2 * WIDTH : 3 * WIDTH] = jnp.where(low, second, turned[1])
    out_ref[:, 3 * WIDTH : 4 * WIDTH] = jnp.where(low, third, down)
    ratio_ref[...] = ratio_in[0:1, 0:1]


def place(turns, inner, turned, landed, ratio):
    rows, wide = inner.shape
    tile = rows // PLACE_STEPS
    return pl.pallas_call(
        functools.partial(place_kernel, lax.axis_size("pair") - 1),
        out_shape=(
            jax.ShapeDtypeStruct((rows, 2 * wide), jnp.float32),
            jax.ShapeDtypeStruct((1, 1), jnp.float32),
        ),
        grid=(PLACE_STEPS,),
        in_specs=[
            pl.BlockSpec(turns.shape, lambda g: (0, 0, 0)),
            pl.BlockSpec((tile, wide), lambda g: (g, 0)),
            pl.BlockSpec((2, tile, WIDTH), lambda g: (0, g, 0)),
            pl.BlockSpec((2, tile, WIDTH), lambda g: (0, lax.rem(g, PLACE_STEPS // 2), 0)),
            pl.BlockSpec((8, WIDTH), lambda g: (0, 0)),
        ],
        out_specs=(
            pl.BlockSpec((tile, 2 * wide), lambda g: (g, 0)),
            pl.BlockSpec((1, 1), lambda g: (0, 0)),
        ),
    )(turns, inner, turned, landed, ratio)


def on_device(r_factor, block_slots):
    turned, landed, inner, grams, ratio = spread(r_factor, block_slots)
    rotated, ratio = place(rotations(grams), inner, turned, landed, ratio)
    return (rotated, ratio.reshape(()))


def solution(mesh):
    in_specs = (P(("row", "pair"), None), P())
    out_specs = (P("row", "pair"), P())
    return jax.shard_map(
        on_device, mesh=mesh, in_specs=in_specs, out_specs=out_specs, check_vma=False
    )
```

time: 107 us -> 109 us (1.019)
  Pallas kernels: 106 us -> 108 us
    pallas_call x3 -> x2, Pallas kernels: 101 us -> 104 us  [the longest x1 97 us: spread(): pl.pallas_call(functools.partial(spread_kernel, xs, ys, zs), out_shape=(f...]
where the time goes in v4:
time: 109 us; the launch traced here: 108 us
  Pallas kernels  108 us (99%)
    pallas_call x1, Pallas kernels, spread(): pl.pallas_call(functools.partial(spread_kernel, xs, ys, zs), out_shape=(f...  97 us
    pallas_call x1, Pallas kernels, rotations(): pl.pallas_call(rotation_kernel, out_shape=jax.ShapeDtypeStruct((pairs, WI...  7.08 us
    pallas_call x1, Pallas kernels, place(): pl.pallas_call(functools.partial(place_kernel, lax.axis_size('pair') - 1)...  3.62 us

profile of v4, /device:TPU:1, one launch (start us, length us, event | category | flops | bytes accessed | tf_op | source)
XLA Modules:
  0.0 108.4 jit_solution(17988283449063226888)
XLA Ops:
  0.6 97.0 %shard_map.41 = (f32[2,1024,128]{2,1,0:T(8,128)}, f32[2,512,128]{2,1,0:T(8,128)}, f32[1024,256]{1,0:T(8,128)}, f32[256,128]{1,0:T(8,128)}, f32[8,128]{1,0:T(8,128)}) custom-call(s32[256]{0:T(256)} %slots_ref.1, f32[32,16384]{1,0:T(8,128)} %r_hbm.1), custom_call_target="tpu_custom_call" | custom-call | tf_op jit(solution)/shard_map/pallas_call | solution.py:393
  97.7 7.1 %shard_map.42.v_ref = f32[2,128,128]{2,1,0:T(8,128)} custom-call(f32[256,128]{1,0:T(8,128)} %get-tuple-element.9.g_ref), custom_call_target="tpu_custom_call" | custom-call | tf_op jit(solution)/shard_map/pallas_call | solution.py:476
  104.8 3.6 %shard_map.43 = (f32[1024,512]{1,0:T(8,128)}, f32[1,1]{1,0:T(1,128)}) custom-call(f32[2,128,128]{2,1,0:T(8,128)} %shard_map.42.v_ref, f32[1024,256]{1,0:T(8,128)} %get-tuple-element.10.x_ref, f32[2,1024,128]{2,1,0:T(8,128)} %get-tuple-element.11.turned, f32[2,512,128]{2,1,0:T(8,128)} %get-tuple-element.12.landed, f32[8,128]{1,0:T(8,128)} %get-tuple-element.13.ratio_in), custom_call_target="tpu_custom_call" | custom-call | tf_op jit(solution)/shard_map/pallas_call | solution.py:508

commit v5 on v4

--- a/solution.py
+++ b/solution.py
@@ -12,10 +12,10 @@
 WIDTH = 2 * BLOCK
 MESH = pl.DeviceIdType.MESH
 HIGHEST = lax.Precision.HIGHEST
-NEUMANN_TOL = 1e-8
+SERIES_TOL = 3e-8
 X_CHIPS = 4
 EARLY = 8
-FACTORS = 12
+FACTORS = 8
 PLACE_STEPS = 2
 
 
@@ -51,10 +51,13 @@
     state[WIDTH:, :] = eye - scale * (eye - square)
 
 
-def series_step(state):
+def series_step(state, reach, unit):
+    square = reach * reach
+    scale = 2.0 / (2.0 - square)
     both = mm(state[...], state[WIDTH:, :])
-    state[0:WIDTH, :] = state[0:WIDTH, :] + both[0:WIDTH]
-    state[WIDTH:, :] = both[WIDTH:]
+    state[0:WIDTH, :] = scale * (state[0:WIDTH, :] + both[0:WIDTH])
+    state[WIDTH:, :] = scale * both[WIDTH:] + jnp.where(unit, 1.0 - scale, 0.0)
+    return square / (2.0 - square)
 
 
 def sweep_end(sweep, tall, state):
@@ -172,7 +175,9 @@
 
     def finish(s):
         def body(k, carry):
-            send(s, k).wait()
+            send(s, k).wait_recv()
+            if s == 1:
+                send(s, k).wait_send()
             return carry
 
         return body
@@ -181,11 +186,17 @@
     pl.semaphore_wait(barrier, xs + zs - 1 + count - 1)
     lax.fori_loop(1, EARLY, start(0), 0)
     lax.fori_loop(EARLY, count, both(0), 0)
-    for s in range(1, steps):
-        lax.fori_loop(1, count, both(s), 0)
     for s in range(steps):
         for i in range(2):
             held[s, here, i * WIDTH : (i + 1) * WIDTH] = piece(me, s, i)
+
+    def follow(k, carry):
+        arrange(1)(k, carry)
+        send(0, k).wait_send()
+        send(1, k).start()
+        return carry
+
+    lax.fori_loop(1, count, follow, 0)
 
     def gram(s, i):
         cols = held[s, :, pl.ds(pl.multiple_of(i * WIDTH, WIDTH), WIDTH)]
@@ -214,11 +225,10 @@
             bound = 0.5 * jnp.sum(cells, axis=1, keepdims=True)
             series_start(state, skew, mm(skew, skew), bound, unit)
 
-            def factor(k, carry):
-                series_step(state)
-                return carry
-
-            lax.fori_loop(0, FACTORS, factor, 0)
+            def factor(k, reach):
+                return series_step(state, reach, unit)
+
+            lax.fori_loop(0, FACTORS, factor, bound / (2.0 + bound))
             sweep_end(sweep, tall, state)
         v_pair[core] = tall[WIDTH:, :]
         swap = pltpu.make_async_remote_copy(
@@ -449,20 +459,23 @@
     for p in range(pairs):
         tall[p, 0:WIDTH, :] = g_ref[p * WIDTH : (p + 1) * WIDTH, :]
     for sweep in range(ITERS):
-        ratio = jnp.zeros((), jnp.float32)
+        most = jnp.zeros((), jnp.float32)
+        work = []
         for p in range(pairs):
             skew = skew_of(tall[p, 0:WIDTH, :], unit)
             square = mm(skew, skew)
             bound = jnp.max(jnp.sum(jnp.abs(square), axis=0, keepdims=True))
-            series_start(state.at[p], skew, square, bound, unit)
-            ratio = jnp.maximum(ratio, bound / (2.0 + bound))
-
-        def step(carry):
+            work.append((skew, square))
+            most = jnp.maximum(most, bound)
+        for p in range(pairs):
+            series_start(state.at[p], *work[p], most, unit)
+
+        def step(reach):
             for p in range(pairs):
-                series_step(state.at[p])
-            return carry * carry
-
-        lax.while_loop(lambda left: left > NEUMANN_TOL, step, ratio)
+                after = series_step(state.at[p], reach, unit)
+            return after
+
+        lax.while_loop(lambda reach: reach > SERIES_TOL, step, most / (2.0 + most))
         for p in range(pairs):
             sweep_end(sweep, tall.at[p], state.at[p])
     for p in range(pairs):

time: 109 us -> 106 us (0.972)
  Pallas kernels: 108 us -> 105 us
    pallas_call x1, Pallas kernels: 97 us -> 94 us  [spread(): pl.pallas_call(functools.partial(spread_kernel, xs, ys, zs), out_shape=(f...]
where the time goes in v5:
time: 106 us; the launch traced here: 105 us
  Pallas kernels  105 us (99%)
    pallas_call x1, Pallas kernels, spread(): pl.pallas_call(functools.partial(spread_kernel, xs, ys, zs), out_shape=(f...  94 us
    pallas_call x1, Pallas kernels, rotations(): pl.pallas_call(rotation_kernel, out_shape=jax.ShapeDtypeStruct((pairs, WI...  7.16 us
    pallas_call x1, Pallas kernels, place(): pl.pallas_call(functools.partial(place_kernel, lax.axis_size('pair') - 1)...  3.62 us

profile of v5, /device:TPU:1, one launch (start us, length us, event | category | flops | bytes accessed | tf_op | source)
XLA Modules:
  0.0 105.4 jit_solution(7243553660484665126)
XLA Ops:
  0.6 94.0 %shard_map.41 = (f32[2,1024,128]{2,1,0:T(8,128)}, f32[2,512,128]{2,1,0:T(8,128)}, f32[1024,256]{1,0:T(8,128)}, f32[256,128]{1,0:T(8,128)}, f32[8,128]{1,0:T(8,128)}) custom-call(s32[256]{0:T(256)} %slots_ref.1, f32[32,16384]{1,0:T(8,128)} %r_hbm.1), custom_call_target="tpu_custom_call" | custom-call | tf_op jit(solution)/shard_map/pallas_call | solution.py:403
  94.6 7.2 %shard_map.42.v_ref = f32[2,128,128]{2,1,0:T(8,128)} custom-call(f32[256,128]{1,0:T(8,128)} %get-tuple-element.9.g_ref), custom_call_target="tpu_custom_call" | custom-call | tf_op jit(solution)/shard_map/pallas_call | solution.py:489
  101.7 3.6 %shard_map.43 = (f32[1024,512]{1,0:T(8,128)}, f32[1,1]{1,0:T(1,128)}) custom-call(f32[2,128,128]{2,1,0:T(8,128)} %shard_map.42.v_ref, f32[1024,256]{1,0:T(8,128)} %get-tuple-element.10.x_ref, f32[2,1024,128]{2,1,0:T(8,128)} %get-tuple-element.11.turned, f32[2,512,128]{2,1,0:T(8,128)} %get-tuple-element.12.landed, f32[8,128]{1,0:T(8,128)} %get-tuple-element.13.ratio_in), custom_call_target="tpu_custom_call" | custom-call | tf_op jit(solution)/shard_map/pallas_call | solution.py:521

commit v6 on v5

--- a/solution.py
+++ b/solution.py
@@ -16,6 +16,7 @@
 X_CHIPS = 4
 EARLY = 8
 FACTORS = 8
+BEFORE = 2
 PLACE_STEPS = 2
 
 
@@ -217,30 +218,30 @@
 
     unit = unit_mask()
 
-    def rotate_edges():
-        tall[0:WIDTH, :] = full[0]
-        for sweep in range(ITERS):
-            skew = skew_of(tall[0:WIDTH, :], unit)
-            cells = jnp.sum(skew * skew, axis=0, keepdims=True)
-            bound = 0.5 * jnp.sum(cells, axis=1, keepdims=True)
-            series_start(state, skew, mm(skew, skew), bound, unit)
-
-            def factor(k, reach):
-                return series_step(state, reach, unit)
-
-            lax.fori_loop(0, FACTORS, factor, bound / (2.0 + bound))
-            sweep_end(sweep, tall, state)
-        v_pair[core] = tall[WIDTH:, :]
-        swap = pltpu.make_async_remote_copy(
-            src_ref=v_pair.at[core],
-            dst_ref=v_pair.at[core],
-            send_sem=v_send,
-            recv_sem=v_recv,
-            device_id={"row": other},
-            device_id_type=MESH,
-        )
-        swap.start()
-        swap.wait()
+    def edge_sweep(sweep):
+        if sweep == 0:
+            tall[0:WIDTH, :] = full[0]
+        skew = skew_of(tall[0:WIDTH, :], unit)
+        cells = jnp.sum(skew * skew, axis=0, keepdims=True)
+        bound = 0.5 * jnp.sum(cells, axis=1, keepdims=True)
+        series_start(state, skew, mm(skew, skew), bound, unit)
+
+        def factor(k, reach):
+            return series_step(state, reach, unit)
+
+        lax.fori_loop(0, FACTORS, factor, bound / (2.0 + bound))
+        sweep_end(sweep, tall, state)
+
+    v_swap = pltpu.make_async_remote_copy(
+        src_ref=v_pair.at[core],
+        dst_ref=v_pair.at[core],
+        send_sem=v_send,
+        recv_sem=v_recv,
+        device_id={"row": other},
+        device_id_type=MESH,
+    )
+
+    def send_edges():
         edge_rows = turned.shape[1] // 2
         lane = lanes((edge_rows, WIDTH))
         for side in range(2):
@@ -250,6 +251,7 @@
             value = turned.at[side]
             rolled = pltpu.roll(value[edge_rows:, :], BLOCK, 1)
             packed[side] = jnp.where(keep, value[0:edge_rows, :], rolled)
+            edge_copy(side).start()
 
     own = pl.ds(pl.multiple_of(z * chunk, chunk), chunk)
     for s in range(steps):
@@ -257,8 +259,6 @@
         if s == 1:
             save = pltpu.make_async_copy(held.at[s], x_hbm, save_sem.at[2])
             save.start()
-            for side in range(2):
-                edge_copy(side).start()
         gram(s, 1 - core)
         swap = pltpu.make_async_remote_copy(
             src_ref=part.at[s, pl.ds(pl.multiple_of((1 - core) * half, half), half)],
@@ -286,6 +286,10 @@
 
         for k in range(1, zs):
             scatter(k).start()
+        if s == 1:
+            for sweep in range(BEFORE, ITERS):
+                edge_sweep(sweep)
+            v_pair[core] = tall[WIDTH:, :]
         for k in range(1, zs):
             scatter(k).wait()
         total = mine[s, own, :]
@@ -305,10 +309,15 @@
 
         for k in range(1, zs):
             gather(k).start()
+        if s == 1:
+            v_swap.start()
+            v_swap.wait()
+            send_edges()
         for k in range(1, zs):
             gather(k).wait()
         if s == 0:
-            rotate_edges()
+            for sweep in range(BEFORE):
+                edge_sweep(sweep)
 
     pair_g = part.at[0]
     own_g = pl.ds(pl.multiple_of(core * half, half), half)

time: 106 us -> 103 us (0.972)
  Pallas kernels: 105 us -> 102 us
    pallas_call x1, Pallas kernels: 94 us -> 91.4 us  [spread(): pl.pallas_call(functools.partial(spread_kernel, xs, ys, zs), out_shape=(f...]
where the time goes in v6:
time: 103 us
  Pallas kernels  102 us (99%)
    pallas_call x1, Pallas kernels, spread(): pl.pallas_call(functools.partial(spread_kernel, xs, ys, zs), out_shape=(f...  91.4 us
    pallas_call x1, Pallas kernels, rotations(): pl.pallas_call(rotation_kernel, out_shape=jax.ShapeDtypeStruct((pairs, WI...  7.17 us
    pallas_call x1, Pallas kernels, place(): pl.pallas_call(functools.partial(place_kernel, lax.axis_size('pair') - 1)...  3.61 us

profile of v6, /device:TPU:1, one launch (start us, length us, event | category | flops | bytes accessed | tf_op | source)
XLA Modules:
  0.0 102.8 jit_solution(9842759983351066781)
XLA Ops:
  0.6 91.4 %shard_map.41 = (f32[2,1024,128]{2,1,0:T(8,128)}, f32[2,512,128]{2,1,0:T(8,128)}, f32[1024,256]{1,0:T(8,128)}, f32[256,128]{1,0:T(8,128)}, f32[8,128]{1,0:T(8,128)}) custom-call(s32[256]{0:T(256)} %slots_ref.1, f32[32,16384]{1,0:T(8,128)} %r_hbm.1), custom_call_target="tpu_custom_call" | custom-call | tf_op jit(solution)/shard_map/pallas_call | solution.py:412
  92.0 7.2 %shard_map.42.v_ref = f32[2,128,128]{2,1,0:T(8,128)} custom-call(f32[256,128]{1,0:T(8,128)} %get-tuple-element.9.g_ref), custom_call_target="tpu_custom_call" | custom-call | tf_op jit(solution)/shard_map/pallas_call | solution.py:498
  99.2 3.6 %shard_map.43 = (f32[1024,512]{1,0:T(8,128)}, f32[1,1]{1,0:T(1,128)}) custom-call(f32[2,128,128]{2,1,0:T(8,128)} %shard_map.42.v_ref, f32[1024,256]{1,0:T(8,128)} %get-tuple-element.10.x_ref, f32[2,1024,128]{2,1,0:T(8,128)} %get-tuple-element.11.turned, f32[2,512,128]{2,1,0:T(8,128)} %get-tuple-element.12.landed, f32[8,128]{1,0:T(8,128)} %get-tuple-element.13.ratio_in), custom_call_target="tpu_custom_call" | custom-call | tf_op jit(solution)/shard_map/pallas_call | solution.py:530

commit v7 on v6

--- a/solution.py
+++ b/solution.py
@@ -16,6 +16,7 @@
 X_CHIPS = 4
 EARLY = 8
 FACTORS = 8
+AT_LEAST = 3
 BEFORE = 2
 PLACE_STEPS = 2
 
@@ -229,7 +230,7 @@
         def factor(k, reach):
             return series_step(state, reach, unit)
 
-        lax.fori_loop(0, FACTORS, factor, bound / (2.0 + bound))
+        lax.fori_loop(0, FACTORS, factor, bound / (2.0 + bound), unroll=4)
         sweep_end(sweep, tall, state)
 
     v_swap = pltpu.make_async_remote_copy(
@@ -484,7 +485,10 @@
                 after = series_step(state.at[p], reach, unit)
             return after
 
-        lax.while_loop(lambda reach: reach > SERIES_TOL, step, most / (2.0 + most))
+        reach = most / (2.0 + most)
+        for _ in range(AT_LEAST):
+            reach = step(reach)
+        lax.while_loop(lambda left: left > SERIES_TOL, step, reach)
         for p in range(pairs):
             sweep_end(sweep, tall.at[p], state.at[p])
     for p in range(pairs):

time: 103 us -> 105 us (1.019)
    pallas_call x1, Pallas kernels: 7.17 us -> 8.35 us  [rotations(): pl.pallas_call(rotation_kernel, out_shape=jax.ShapeDtypeStruct((pairs, WI...]
where the time goes in v7:
time: 105 us; the launch traced here: 104 us
  Pallas kernels  103 us (98%)
    pallas_call x1, Pallas kernels, spread(): pl.pallas_call(functools.partial(spread_kernel, xs, ys, zs), out_shape=(f...  91.4 us
    pallas_call x1, Pallas kernels, rotations(): pl.pallas_call(rotation_kernel, out_shape=jax.ShapeDtypeStruct((pairs, WI...  8.35 us
    pallas_call x1, Pallas kernels, place(): pl.pallas_call(functools.partial(place_kernel, lax.axis_size('pair') - 1)...  3.61 us

profile of v7, /device:TPU:1, one launch (start us, length us, event | category | flops | bytes accessed | tf_op | source)
XLA Modules:
  0.0 104.0 jit_solution(14607835251823527423)
XLA Ops:
  0.6 91.4 %shard_map.41 = (f32[2,1024,128]{2,1,0:T(8,128)}, f32[2,512,128]{2,1,0:T(8,128)}, f32[1024,256]{1,0:T(8,128)}, f32[256,128]{1,0:T(8,128)}, f32[8,128]{1,0:T(8,128)}) custom-call(s32[256]{0:T(256)} %slots_ref.1, f32[32,16384]{1,0:T(8,128)} %r_hbm.1), custom_call_target="tpu_custom_call" | custom-call | tf_op jit(solution)/shard_map/pallas_call | solution.py:413
  92.0 8.3 %shard_map.42.v_ref = f32[2,128,128]{2,1,0:T(8,128)} custom-call(f32[256,128]{1,0:T(8,128)} %get-tuple-element.9.g_ref), custom_call_target="tpu_custom_call" | custom-call | tf_op jit(solution)/shard_map/pallas_call | solution.py:502
  100.4 3.6 %shard_map.43 = (f32[1024,512]{1,0:T(8,128)}, f32[1,1]{1,0:T(1,128)}) custom-call(f32[2,128,128]{2,1,0:T(8,128)} %shard_map.42.v_ref, f32[1024,256]{1,0:T(8,128)} %get-tuple-element.10.x_ref, f32[2,1024,128]{2,1,0:T(8,128)} %get-tuple-element.11.turned, f32[2,512,128]{2,1,0:T(8,128)} %get-tuple-element.12.landed, f32[8,128]{1,0:T(8,128)} %get-tuple-element.13.ratio_in), custom_call_target="tpu_custom_call" | custom-call | tf_op jit(solution)/shard_map/pallas_call | solution.py:534
